TPU v7x, 32 devices: a whole 2x2x4 slice. The times are simulated.
32 devices in a mesh: dp: 16 (over z, y, x), mp: 2 (over core).
Axes of the slice: x: 2, y: 2, z: 4, core: 2. Of those that a mesh axis runs over, the one named last changes fastest.
Arguments:
- grads: bfloat16 [16384, 16384], P('dp', 'mp'), may hold values from -6 to 6
- scales: float32 [128, 16384], P('mp', 'dp'), may hold values from 0.25 to 4
- example_group: int32 [16, 1024], P('dp'), may hold values from 0 to 127, never falling along the last dimension, each value on 1 to 32 neighbouring positions
- group_slot: int32 [2048], P('dp'), may hold values from 0 to 2047, as said below
- inv_hess: bfloat16 [16384, 16384], P('mp', 'dp'), may hold values from -0.046875 to 0.046875
- queries: bfloat16 [512, 16384], P(None, 'mp'), may hold values from -0.029907227 to 0.029907227
Outputs:
- scores: float32 [2048, 512], P('dp', 'mp')
Inputs may be any that keep to these rules, and one draw needn't show every extreme that they name: `group_slot`: A permutation of the 2048 rows. The groups of one block of 128 (one index of dp) put at most 16 groups into the rows of any one owner block of 128 output rows, and exactly 16 into some owner block.
All inputs are finite; a program needn't handle non-finite values.
Results may differ from a plain program's by a relative error of at most 0.0049.
Values may be sent and summed in bfloat16 or wider, within the bound.
No kernel may reach another device: no remote copies, remote signals or barrier semaphores. Data moves between devices by JAX's collectives and lax.ppermute only.
A program may use at most 128 MiB of HBM per device.

v0:
```python
import jax
import jax.numpy as jnp
from jax import lax
from jax.sharding import PartitionSpec as P

QBLOCK = 128
GRP_DEV = 128


def spread_2(value, axis, source):
    kept = jnp.where(lax.axis_index(axis) == source, value, 0).astype(value.dtype)
    return lax.psum(kept, axis)


def contract(left, right):
    return lax.dot_general(
        left, right, (((1,), (1,)), ((), ())), preferred_element_type=jnp.float32
    )


def local(grads, scales, example_group, group_slot, inv_hess, queries):
    devices = lax.axis_size("dp")
    lanes = lax.axis_size("mp")
    spread = devices // lanes
    ex_rows, width = grads.shape
    query_count = queries.shape[0]
    share = query_count // lanes
    dequant = (
        (grads.reshape(ex_rows, width // QBLOCK, QBLOCK) * jnp.transpose(scales)[:, :, None])
        .astype(jnp.bfloat16)
        .reshape(ex_rows, width)
    )
    onehot = (jnp.arange(GRP_DEV, dtype=jnp.int32)[:, None] == example_group[0][None, :]).astype(
        jnp.bfloat16
    )
    group_grad = jnp.dot(onehot, dequant, preferred_element_type=jnp.float32).astype(jnp.bfloat16)
    query_block = lax.psum_scatter(
        jnp.dot(queries, inv_hess, preferred_element_type=jnp.float32),
        "mp",
        scatter_dimension=0,
        tiled=True,
    ).astype(jnp.bfloat16)
    column_block = lax.all_gather(query_block, "mp", axis=0, tiled=True)
    first_root = spread * lax.axis_index("mp")
    received = [spread_2(column_block, "dp", first_root + offset) for offset in range(spread)]
    precond = jnp.concatenate(received, axis=1)
    partial_value = contract(group_grad, precond)
    mine = lax.psum_scatter(partial_value, "mp", scatter_dimension=1, tiled=True)
    owner = group_slot // GRP_DEV
    inside = group_slot % GRP_DEV
    local_index = jnp.arange(GRP_DEV, dtype=jnp.int32)
    earlier = (owner[:, None] == owner[None, :]) & (local_index[None, :] < local_index[:, None])
    order_rank = jnp.sum(earlier.astype(jnp.int32), axis=1)
    capacity = 2 * GRP_DEV // devices
    buffer_row = owner * capacity + order_rank
    outgoing = jnp.zeros((devices * capacity, share), jnp.float32).at[buffer_row].set(mine)
    targets = (
        jnp.full((devices * capacity,), float(GRP_DEV), jnp.float32)
        .at[buffer_row]
        .set(inside.astype(jnp.float32))
    )
    arrived, arrived_rows = (
        lax.all_to_all(
            outgoing.reshape(devices, capacity, share),
            "dp",
            split_axis=0,
            concat_axis=0,
            tiled=True,
        ),
        lax.all_to_all(
            targets.reshape(devices, capacity), "dp", split_axis=0, concat_axis=0, tiled=True
        ),
    )
    place_rows = arrived_rows.reshape(-1).astype(jnp.int32)
    filled = (
        jnp.zeros((GRP_DEV + 1, share), jnp.float32).at[place_rows].add(arrived.reshape(-1, share))
    )
    return filled[:GRP_DEV]


def solution(mesh):
    in_specs = (P("dp", "mp"), P("mp", "dp"), P("dp", None), P("dp"), P("mp", "dp"), P(None, "mp"))
    out_specs = P("dp", "mp")
    return jax.shard_map(local, mesh=mesh, in_specs=in_specs, out_specs=out_specs, check_vma=False)
```

profile of v0, /device:TPU:0, one launch (start us, length us, event | category | flops | bytes accessed | tf_op | source)
XLA Modules:
  0.0 409.0 jit_solution(7792471635446050200)
XLA Ops:
  6.5 15.9 %fusion.19 = f32[512,1024]{1,0:T(8,128)} fusion(bf16[512,8192]{1,0:T(8,128)(2,1)} %param.11, bf16[8192,1024]{1,0:T(8,128)(2,1)} %param.10), kind=kOutput, calls=%fused_computation.44 | convolution fusion | flops 8589934592 | bytes 27262976 | tf_op jit(solution)/shard_map/dot_general | solution.py:38
  22.5 12.6 %reduce-scatter.3.cloned.1.call-done = f32[256,1024]{1,0:T(8,128)} async-done(((f32[512,1024]{1,0:T(8,128)}), f32[256,1024]{1,0:T(8,128)}) %reduce-scatter.3.cloned.1.call-update) | async-done | bytes 1048592 | tf_op jit(solution)/shard_map/reduce_scatter | solution.py:37
  35.1 2.1 convert_element_type.50
  37.3 10.4 %all-gather.2.cloned.1.call-done = bf16[512,1024]{1,0:T(8,128)(2,1)} async-done(((bf16[256,1024]{1,0:T(8,128)(2,1)}), bf16[512,1024]{1,0:T(8,128)(2,1)}) %all-gather.2.cloned.1.call-update) | async-done | bytes 1048592 | tf_op jit(solution)/shard_map/all_gather | solution.py:43
  47.7 4.5 %broadcast_select_fusion = (bf16[512,1024]{1,0:T(8,128)(2,1)}, bf16[512,1024]{1,0:T(8,128)(2,1)}, bf16[512,1024]{1,0:T(8,128)(2,1)}, bf16[512,1024]{1,0:T(8,128)...) fusion(bf16[512,1024]{1,0:T(8,128)(2,1)} %all-gather.2.cloned.1, ...), kind=kLoop, calls=%fused_computation.8 | loop fusion | flops 4194304 | bytes 9437192 | tf_op jit(solution)/shard_map/jit(_where)/select_n | solution.py:11
  52.5 259.1 %all-reduce.3.cloned.1.call-done = (bf16[512,1024]{1,0:T(8,128)(2,1)}, bf16[512,1024]{1,0:T(8,128)(2,1)}, bf16[512,1024]{1,0:T(8,128)(2,1)}, bf16[512,1024]{1,0:...) async-done(((bf16[512,1024]{1,0:T(8,128)(2,1)}, bf16[512,1024]{1,0:T(8,128)(2,1)}, ...) | async-done | bytes 8388624 | tf_op jit(solution)/shard_map/psum | solution.py:12
  311.5 2.4 constant_dynamic-update-slice_fusion.7
  314.0 2.3 constant_dynamic-update-slice_fusion.6
  316.3 2.3 constant_dynamic-update-slice_fusion.5
  318.6 2.3 constant_dynamic-update-slice_fusion.4
  320.9 1.1 constant_dynamic-update-slice_fusion.3
  322.0 1.1 constant_dynamic-update-slice_fusion.2
  323.0 1.1 constant_dynamic-update-slice_fusion.1
  324.1 1.0 constant_dynamic-update-slice_fusion
  325.2 21.3 %mul.19 = f32[1024,64,128]{2,1,0:T(8,128)} broadcast(f32[1024,64]{1,0:T(8,128)S(1)} %copy.9), dimensions={0,1} | broadcast | bytes 33816576 | tf_op jit(solution)/shard_map/mul | solution.py:29
  346.5 27.6 %fusion.7 = f32[128,512]{1,0:T(8,128)} fusion(bf16[512,8192]{1,0:T(8,128)(2,1)} %constant_dynamic-update-slice_fusion, f32[128,8,64,128]{3,2,1,0:T(8,128)} %bitcast.18, bf16[1024,8192]{1,0:T(8,128)(2,1)} %param.6, s32[1024]{0:T(1024)S(1)} %bitcast.21), kind=kOutput, calls=%fused_computation.7 | convolution fusion | flops 3247570944 | bytes 58986496 | tf_op jit(solution)/shard_map/dot_general | solution.py:16
  374.3 1.0 scatter_custom_fusion
  375.3 0.7 all_to_all.9
  376.0 4.6 %all-to-all-start = ((f32[16,1,16]{2,1,0:T(1,128)}), f32[16,1,16]{2,1,0:T(1,128)S(1)}, u32[]{:S(2)}, u32[]{:S(2)}) async-start(f32[16,1,16]{2,1,0:T(1,128)} %all_to_all.9), calls=%async_computation | async-start | bytes 16384 | tf_op jit(solution)/shard_map/all_to_all | solution.py:70
  381.0 2.0 scatter_custom_fusion.1
  383.0 4.8 %all-to-all-done = f32[16,1,16]{2,1,0:T(1,128)S(1)} async-done(((f32[16,1,16]{2,1,0:T(1,128)}), f32[16,1,16]{2,1,0:T(1,128)S(1)}, u32[]{:S(2)}, u32[]{:S(2)}) %all-to-all-start) | async-done | bytes 1056 | tf_op jit(solution)/shard_map/all_to_all | solution.py:70
  387.8 3.5 all-to-all-start.1
  391.5 8.3 %all-to-all-done.1 = f32[16,16,256]{2,1,0:T(8,128)S(1)} async-done(((f32[16,16,256]{2,1,0:T(8,128)}), f32[16,16,256]{2,1,0:T(8,128)S(1)}, u32[]{:S(2)}, u32[]{:S(2)}) %all-to-all-start.1) | async-done | bytes 262176 | tf_op jit(solution)/shard_map/all_to_all | solution.py:63
  399.8 2.0 scatter_custom_fusion.2
  (31 shorter events, 1.8 us)
Async XLA Ops:
  6.5 28.6 %reduce-scatter.3.cloned.1.call-start = ((), (), s32[]{:S(2)}) async-start(), calls=%async_computation.4 | async-start | bytes 3145728 | tf_op jit(solution)/shard_map/reduce_scatter | solution.py:37
  22.5 25.2 %all-gather.2.cloned.1.call-start = ((), (), s32[]{:S(2)}) async-start(), calls=%async_computation.5 | async-start | bytes 1572864 | tf_op jit(solution)/shard_map/all_gather | solution.py:43
  37.2 274.3 %all-reduce.3.cloned.1.call-start = ((), (), s32[]{:S(2)}) async-start(), calls=%async_computation.7 | async-start | bytes 16777216 | tf_op jit(solution)/shard_map/psum | solution.py:12
  37.3 15.0 %copy-start.4 = (f32[64,1024]{1,0:T(8,128)S(1)}, f32[64,1024]{1,0:T(8,128)}, u32[]{:S(2)}) copy-start(f32[64,1024]{1,0:T(8,128)} %param.7) | copy-start | bytes 786436
  52.2 328.8 %reduce-scatter.5.cloned.1.call-start = ((), (), s32[]{:S(2)}) async-start(), calls=%async_computation.6 | async-start | bytes 393216 | tf_op jit(solution)/shard_map/reduce_scatter | solution.py:48
  311.5 9.4 %copy-start.3 = (bf16[512,1024]{1,0:T(8,128)(2,1)S(1)}, bf16[512,1024]{1,0:T(8,128)(2,1)}, u32[]{:S(2)}) copy-start(bf16[512,1024]{1,0:T(8,128)(2,1)} %get-tuple-element.9) | copy-start | bytes 3145732
  311.5 10.5 %copy-start.2 = (bf16[512,1024]{1,0:T(8,128)(2,1)S(1)}, bf16[512,1024]{1,0:T(8,128)(2,1)}, u32[]{:S(2)}) copy-start(bf16[512,1024]{1,0:T(8,128)(2,1)} %get-tuple-element.10) | copy-start | bytes 3145732
  311.5 11.5 %copy-start.1 = (bf16[512,1024]{1,0:T(8,128)(2,1)S(1)}, bf16[512,1024]{1,0:T(8,128)(2,1)}, u32[]{:S(2)}) copy-start(bf16[512,1024]{1,0:T(8,128)(2,1)} %get-tuple-element.11) | copy-start | bytes 3145732
  311.5 12.6 %copy-start = (bf16[512,1024]{1,0:T(8,128)(2,1)S(1)}, bf16[512,1024]{1,0:T(8,128)(2,1)}, u32[]{:S(2)}) copy-start(bf16[512,1024]{1,0:T(8,128)(2,1)} %get-tuple-element.12) | copy-start | bytes 3145732
  325.2 21.3 %copy-start.5 = (s32[1,1024]{1,0:T(1,128)S(1)}, s32[1,1024]{1,0:T(1,128)}, u32[]{:S(2)}) copy-start(s32[1,1024]{1,0:T(1,128)} %param.8) | copy-start | bytes 12292
  346.5 27.6 %copy-start.6 = (s32[128]{0:T(128)S(1)}, s32[128]{0:T(128)}, u32[]{:S(2)}) copy-start(s32[128]{0:T(128)} %param.9) | copy-start | bytes 1540
  376.0 11.8 %all-to-all-start = ((f32[16,1,16]{2,1,0:T(1,128)}), f32[16,1,16]{2,1,0:T(1,128)S(1)}, u32[]{:S(2)}, u32[]{:S(2)}) async-start(f32[16,1,16]{2,1,0:T(1,128)} %all_to_all.9), calls=%async_computation | async-start | bytes 16384 | tf_op jit(solution)/shard_map/all_to_all | solution.py:70
  387.8 12.0 %all-to-all-start.1 = ((f32[16,16,256]{2,1,0:T(8,128)}), f32[16,16,256]{2,1,0:T(8,128)S(1)}, u32[]{:S(2)}, u32[]{:S(2)}) async-start(f32[16,16,256]{2,1,0:T(8,128)} %bitcast.3), calls=%async_computation.3 | async-start | bytes 524288 | tf_op jit(solution)/shard_map/all_to_all | solution.py:63
Sparse Core Ops, SparseCore 0:
  22.6 12.4 reduce-scatter.2
  37.3 10.2 all-gather.1
  54.1 257.3 all-reduce.2
  374.2 6.6 reduce-scatter.4
where the time goes:
time: 409 us
  waiting for transfers between devices  296 us (72%)
  matrix products  43.5 us (11%)
  local copies, waits for them, and re-layouts  39.6 us (10%)
  between operations  13.2 us (3%)
  other arithmetic  8.81 us (2%)
  starting transfers between devices  8.22 us (2%)
    psum x1, waiting for transfers between devices, spread_2(): return lax.psum(kept, axis)  259 us
    dot_general x1, matrix products, contract(): lax.dot_general(left, right, (((1,), (1,)), ((), ())), preferred_element_...  27.6 us
    mul x1, local copies, waits for them, and re-layouts, local(): grads.reshape(ex_rows, width // QBLOCK, QBLOCK)  21.3 us
    dot_general x1, matrix products, local(): jnp.dot(queries, inv_hess, preferred_element_type=jnp.float32)  15.9 us
    unnamed x21, local copies, waits for them, and re-layouts  12.6 us
    reduce_scatter x1, waiting for transfers between devices, local(): lax.psum_scatter(jnp.dot(queries, inv_hess, preferred_element_type=jnp.fl...  12.6 us
    all_gather x1, waiting for transfers between devices, local(): column_block = lax.all_gather(query_block, 'mp', axis=0, tiled=True)  10.4 us
    all_to_all x1, waiting for transfers between devices, local(): lax.all_to_all(outgoing.reshape(devices, capacity, share), 'dp', split_ax...  8.35 us
  transfers between devices with their start and end apart: 6, of which 6 were waited for; matrix products, arithmetic and copies ran while one was open for 1% of the time, Pallas kernels for 0%

commit v1 on v0

v1 whole, which is shorter than its diff:
```python
import jax
import jax.numpy as jnp
from jax import lax
from jax.experimental import pallas as pl
from jax.experimental.pallas import tpu as pltpu
from jax.sharding import PartitionSpec as P

QBLOCK = 128
GRP_DEV = 128
AXES = ("dp", "mp")
LANES = 128
TAG = 16


def params(*semantics):
    return pltpu.CompilerParams(dimension_semantics=semantics)


def precond_kernel(place, queries, inv_hess, mine, theirs, left, right, acc, sems, *, cut, blocks):
    width = right.shape[1]
    copies = []
    start = 0
    for i, depth in enumerate(blocks):
        span = pl.ds(start, depth)
        pair = (
            pltpu.make_async_copy(queries.at[:, span], left.at[:, span], sems.at[0, i]),
            pltpu.make_async_copy(
                inv_hess.at[span, pl.ds(cut * width, width)], right.at[span, :], sems.at[1, i]
            ),
        )
        for copy in pair:
            copy.start()
        copies.append((span, pair))
        start += depth
    for i, (span, pair) in enumerate(copies):
        for copy in pair:
            copy.wait()
        product = jnp.dot(left[:, span], right[span, :], preferred_element_type=jnp.float32)
        if i == 0:
            acc[...] = product
        else:
            acc[...] += product
    lane, share = place[2], mine.shape[0]
    mine[...] = acc[pl.ds(lane * share, share), :]
    for other in range(theirs.shape[0]):
        first = jnp.bitwise_xor(lane, other + 1) * share
        theirs[other] = acc[pl.ds(first, share), :]


def precond_part(place, queries, inv_hess, lanes, cut, cuts):
    count, depth = queries.shape
    width = inv_hess.shape[1] // cuts
    share = count // lanes
    unit = depth // 16
    blocks = (unit, unit, 2 * unit, 4 * unit, 4 * unit, 4 * unit)
    whole = pl.BlockSpec(memory_space=pl.ANY)
    return pl.pallas_call(
        lambda *refs: precond_kernel(*refs, cut=cut, blocks=blocks),
        grid_spec=pltpu.PrefetchScalarGridSpec(
            num_scalar_prefetch=1,
            grid=(1,),
            in_specs=[whole, whole],
            out_specs=[
                pl.BlockSpec((share, width), lambda k, _: (0, 0)),
                pl.BlockSpec((lanes - 1, share, width), lambda k, _: (0, 0, 0)),
            ],
            scratch_shapes=[
                pltpu.VMEM((count, depth), queries.dtype),
                pltpu.VMEM((depth, width), inv_hess.dtype),
                pltpu.VMEM((count, width), jnp.float32),
                pltpu.SemaphoreType.DMA((2, len(blocks))),
            ],
        ),
        out_shape=[
            jax.ShapeDtypeStruct((share, width), jnp.float32),
            jax.ShapeDtypeStruct((lanes - 1, share, width), jnp.float32),
        ],
        compiler_params=params("arbitrary"),
        cost_estimate=pl.CostEstimate(
            flops=2 * count * depth * width,
            transcendentals=0,
            bytes_accessed=2 * (count * depth + depth * width),
        ),
    )(place, queries, inv_hess)


def group_kernel(
    place, grads, scales, onehot, tag, out, buffer, sems, *, peer, chips, columns, width, cut
):
    rows = buffer.shape[0]
    groups = onehot.shape[0]
    blocks = cut // QBLOCK
    copies = []
    for c in range(columns):
        column = c * chips + jnp.bitwise_xor(place[1], peer)
        for start in range(0, width, cut):
            at = c * width + start
            copy = pltpu.make_async_copy(
                grads.at[:, pl.ds(pl.multiple_of(column * width + start, LANES), cut)],
                buffer.at[:, pl.ds(at, cut)],
                sems.at[len(copies)],
            )
            copy.start()
            copies.append((copy, at, column, start // QBLOCK))
    out[groups:, :] = jnp.zeros((TAG, out.shape[1]), jnp.bfloat16)
    out[groups:, : tag.shape[1]] = tag[...]
    for copy, at, column, first in copies:
        copy.wait()
        turned = buffer[:, at : at + cut].T.astype(jnp.float32).reshape(blocks, QBLOCK, rows)
        steps = scales[column][first : first + blocks, :]
        dequant = (turned * steps[:, None, :]).astype(jnp.bfloat16).reshape(cut, rows)
        out[:groups, at : at + cut] = lax.dot_general(
            onehot[...], dequant, (((1,), (1,)), ((), ())), preferred_element_type=jnp.float32
        ).astype(jnp.bfloat16)


def group_part(place, grads, scales, onehot, tag, peer, chips, columns, width):
    rows = grads.shape[0]
    groups = onehot.shape[0]
    cut = min(512, width)
    scales = scales.reshape(-1, width // QBLOCK, rows)
    return pl.pallas_call(
        lambda *refs: group_kernel(
            *refs, peer=peer, chips=chips, columns=columns, width=width, cut=cut
        ),
        grid_spec=pltpu.PrefetchScalarGridSpec(
            num_scalar_prefetch=1,
            grid=(1,),
            in_specs=[
                pl.BlockSpec(memory_space=pl.ANY),
                pl.BlockSpec(scales.shape, lambda c, _: (0, 0, 0)),
                pl.BlockSpec(onehot.shape, lambda c, _: (0, 0)),
                pl.BlockSpec(tag.shape, lambda c, _: (0, 0)),
            ],
            out_specs=pl.BlockSpec((groups + TAG, columns * width), lambda c, _: (0, 0)),
            scratch_shapes=[
                pltpu.VMEM((rows, columns * width), grads.dtype),
                pltpu.SemaphoreType.DMA((columns * width // cut,)),
            ],
        ),
        out_shape=jax.ShapeDtypeStruct((groups + TAG, columns * width), jnp.bfloat16),
        compiler_params=params("arbitrary"),
        cost_estimate=pl.CostEstimate(
            flops=2 * groups * rows * columns * width,
            transcendentals=0,
            bytes_accessed=2 * rows * columns * width,
        ),
    )(place, grads, scales, onehot, tag)


def near_kernel(place, *refs, chips, lanes, per_lane, cuts):
    routing, refs = refs[0], refs[1:]
    pieces, refs = refs[: chips * lanes], refs[chips * lanes :]
    out, far, left, total = refs[-4:]
    precond = refs[:-4]
    step, steps = pl.program_id(0), pl.num_programs(0)
    groups = pieces[0].shape[0] - TAG
    source = jnp.bitwise_xor(place[0], step) // per_lane
    holder = jnp.bitwise_xor(source, place[2])
    for lane in range(lanes):

        @pl.when(holder == lane)
        def _():
            for chip in range(chips):
                piece = pieces[lane * chips + chip]
                left[chip * groups : (chip + 1) * groups, :] = piece[:groups, :]

    width = left.shape[1] // cuts
    for hop in range(len(precond) // cuts):

        @pl.when(step == hop)
        def _():
            value = None if hop == 0 else total[...]
            for cut in range(cuts):
                part = lax.dot_general(
                    left[:, cut * width : (cut + 1) * width],
                    precond[hop * cuts + cut][...],
                    (((1,), (1,)), ((), ())),
                    preferred_element_type=jnp.float32,
                )
                value = part if value is None else value + part
            total[...] = value

    @pl.when(step == steps - 1)
    def _():
        far[...] = jnp.dot(
            routing[...], left[...], preferred_element_type=jnp.float32
        ).astype(jnp.bfloat16)
        high = total[...].astype(jnp.bfloat16)
        low = (total[...] - high.astype(jnp.float32)).astype(jnp.bfloat16)
        out[...] = jnp.dot(routing[...], high, preferred_element_type=jnp.float32) + jnp.dot(
            routing[...], low, preferred_element_type=jnp.float32
        )


def near_part(place, routing, pieces, precond, chips, lanes, per_lane, cuts):
    share, width = precond[0].shape
    width = width * cuts
    groups = pieces[0].shape[0] - TAG
    rows = chips * groups
    steps = len(precond) // cuts + 1
    sent = routing.shape[0]

    def column(i, at):
        return (0, jnp.bitwise_xor(at[0], i) % per_lane)

    return pl.pallas_call(
        lambda *refs: near_kernel(
            *refs, chips=chips, lanes=lanes, per_lane=per_lane, cuts=cuts
        ),
        grid_spec=pltpu.PrefetchScalarGridSpec(
            num_scalar_prefetch=1,
            grid=(steps,),
            in_specs=[pl.BlockSpec(routing.shape, lambda i, at: (0, 0))]
            + [pl.BlockSpec((groups + TAG, width), column) for _ in pieces]
            + [pl.BlockSpec(p.shape, lambda i, at: (0, 0)) for p in precond],
            out_specs=[
                pl.BlockSpec((sent, share), lambda i, at: (0, 0)),
                pl.BlockSpec((sent, width), lambda i, at: (0, 0)),
            ],
            scratch_shapes=[
                pltpu.VMEM((rows, width), jnp.bfloat16),
                pltpu.VMEM((rows, share), jnp.float32),
            ],
        ),
        out_shape=[
            jax.ShapeDtypeStruct((sent, share), jnp.float32),
            jax.ShapeDtypeStruct((sent, width), jnp.bfloat16),
        ],
        compiler_params=params("arbitrary"),
        cost_estimate=pl.CostEstimate(
            flops=2 * rows * width * share * (steps - 1),
            transcendentals=0,
            bytes_accessed=2 * rows * width * steps * lanes,
        ),
        name="near",
    )(place, routing, *pieces, *precond)


def local(grads, scales, example_group, group_slot, inv_hess, queries):
    devices = lax.axis_size("dp")
    lanes = lax.axis_size("mp")
    chips = 1 << ((devices.bit_length() - 1) // 2)
    line = devices // chips
    per_lane = line // lanes
    width = inv_hess.shape[1]
    share = queries.shape[0] // lanes
    capacity = 2 * GRP_DEV // devices
    at_line = lax.axis_index("dp") // chips
    at_plane = lax.axis_index("dp") % chips
    place = jnp.stack([at_line, at_plane, lax.axis_index("mp")]).astype(jnp.int32)
    cuts = 1

    def move(value, target):
        pairs = []
        for s in range(line):
            for t in range(chips):
                for m in range(lanes):
                    to = target(s, t, m)
                    if to is not None:
                        a, b, c = to
                        pairs.append(((s * chips + t) * lanes + m, (a * chips + b) * lanes + c))
        return lax.ppermute(value, AXES, pairs)

    def to_lane(value, hop):
        return move(value, lambda s, t, m: (s, t, m ^ hop))

    def to_plane(value, hop):
        return move(value, lambda s, t, m: (s, t ^ hop, m))

    def to_line(value, hop):
        return move(value, lambda s, t, m: (s ^ hop, t, m))

    nearer, farthest = [[] for _ in range(line - 1)], []
    for cut in range(cuts):
        mine, theirs = precond_part(place, queries, inv_hess, lanes, cut, cuts)
        block = mine
        for hop in range(1, lanes):
            block = block + to_lane(theirs[hop - 1], hop)
        block = block.astype(jnp.bfloat16)
        nearer[0].append(block)
        if line == 4:
            two = to_line(block, 2)
            one = to_line(block, 1)
            middle = move(block, lambda s, t, m: (s ^ 3, t, m) if s in (1, 2) else None)
            relayed = move(two, lambda s, t, m: (s ^ 1, t, m) if s in (1, 2) else None)
            nearer[1].append(one)
            nearer[2].append(two)
            farthest.append(middle + relayed)
        else:
            for hop in range(1, line - 1):
                nearer[hop].append(to_line(block, hop))
            farthest.append(to_line(block, line - 1))

    slot = group_slot.reshape(1, GRP_DEV)
    tag = jnp.concatenate([slot // GRP_DEV, slot % GRP_DEV], axis=0)
    tag = jnp.pad(tag, ((0, TAG - 2), (0, 0))).astype(jnp.bfloat16)
    onehot = (
        jnp.arange(GRP_DEV, dtype=jnp.int32)[:, None] == example_group[0][None, :]
    ).astype(jnp.bfloat16)
    pieces = []
    for hop in [*range(chips - 1, 0, -1), 0]:
        made = group_part(place, grads, scales, onehot, tag, hop, chips, per_lane, width)
        pieces.append(to_plane(made, hop) if hop else made)
    pieces = pieces[::-1]
    held = list(pieces)
    for hop in range(1, lanes):
        held += [to_lane(piece, hop) for piece in pieces]

    tags = jnp.stack([p[GRP_DEV : GRP_DEV + 2, :GRP_DEV] for p in pieces]).astype(jnp.int32)
    owner, inside = tags[:, 0], tags[:, 1]
    source = jnp.bitwise_xor(jnp.arange(chips, dtype=jnp.int32), at_plane)[:, None]
    order = jnp.arange(GRP_DEV, dtype=jnp.int32)
    earlier = (owner[:, :, None] == owner[:, None, :]) & (order[None, :] < order[:, None])[None]
    rank = jnp.sum(earlier.astype(jnp.int32), axis=2)
    per_chip = chips * line * capacity
    toward = jnp.bitwise_xor(owner % chips, at_plane)
    row = toward * per_chip + (source * line + owner // chips) * capacity + rank
    rows = jnp.arange(chips * per_chip, dtype=jnp.int32)[:, None]
    routing = (rows == row.reshape(1, -1)).astype(jnp.bfloat16)
    kept = rows[:per_chip] == row.reshape(1, -1)
    meta = GRP_DEV + jnp.sum(
        jnp.where(kept, inside.reshape(1, -1) - GRP_DEV, 0), axis=1, keepdims=True
    )
    meta = jnp.broadcast_to(meta, (per_chip, LANES)).astype(jnp.bfloat16)
    meta = meta.reshape(chips, line, capacity, LANES)

    total, far = near_part(
        place, routing, held, sum(nearer, []), chips, lanes, per_lane, cuts
    )
    for cut in range(cuts):
        columns = slice(cut * width // cuts, (cut + 1) * width // cuts)
        total = total + contract(far[:, columns], farthest[cut])
    sending = total.astype(jnp.bfloat16).reshape(chips, per_chip, share)
    whole = sending[0].astype(jnp.float32)
    for hop in range(1, chips):
        whole = whole + to_plane(sending[hop], hop).astype(jnp.float32)
    whole = whole.astype(jnp.bfloat16).reshape(chips, line, capacity, share)
    whole = jnp.concatenate([whole, meta], axis=3)
    final = []
    for hop in range(line):
        own = lax.dynamic_index_in_dim(whole, jnp.bitwise_xor(at_line, hop), 1, keepdims=False)
        own = own.reshape(chips * capacity, share + LANES)
        final.append(to_line(own, hop) if hop else own)
    final = jnp.concatenate(final, axis=0)
    chosen = (final[:, share:] == jnp.arange(LANES, dtype=jnp.bfloat16)[None, :]).astype(
        jnp.bfloat16
    )
    return lax.dot_general(
        chosen, final[:, :share], (((0,), (0,)), ((), ())), preferred_element_type=jnp.float32
    )


def contract(left, right):
    return lax.dot_general(
        left, right, (((1,), (1,)), ((), ())), preferred_element_type=jnp.float32
    )


def solution(mesh):
    in_specs = (P("dp", "mp"), P("mp", "dp"), P("dp", None), P("dp"), P("mp", "dp"), P(None, "mp"))
    out_specs = P("dp", "mp")

    return jax.shard_map(local, mesh=mesh, in_specs=in_specs, out_specs=out_specs, check_vma=False)
```

time: 409 us -> 121 us (0.30)
  waiting for transfers between devices: 296 us -> 39.2 us
  Pallas kernels: 0 us -> 47.8 us
  matrix products: 43.5 us -> 3.55 us
  local copies, waits for them, and re-layouts: 39.6 us -> 3.91 us
  starting transfers between devices: 8.22 us -> 21.6 us
  between operations: 13.2 us -> 0.27 us
  other arithmetic: 8.81 us -> 4.41 us
    psum x1 -> x0, waiting for transfers between devices: 259 us -> none  [spread_2(): return lax.psum(kept, axis)]
    pallas_call x0 -> x6, Pallas kernels: none -> 47.8 us  [the longest x4 24.3 us: group_part(): pl.pallas_call(lambda *refs: group_kernel(*refs, peer=peer, chips=chips,...]
    ppermute x0 -> x18, waiting for transfers between devices: none -> 39.2 us  [move(): return lax.ppermute(value, AXES, pairs)]
    dot_general x1, matrix products: 27.6 us -> 2.67 us  [contract(): lax.dot_general(left, right, (((1,), (1,)), ((), ())), preferred_element_...]
    ppermute x0 -> x18, starting transfers between devices: none -> 21.6 us  [move(): return lax.ppermute(value, AXES, pairs)]
    mul x1 -> x0, local copies, waits for them, and re-layouts: 21.3 us -> none  [local(): grads.reshape(ex_rows, width // QBLOCK, QBLOCK)]
    dot_general x1, matrix products: 15.9 us -> 0.88 us  [local(): lax.dot_general(chosen, final[:, :share], (((0,), (0,)), ((), ())), prefe...]
    all_to_all x2 -> x0, waiting for transfers between devices: 13.2 us -> none  [the longest x1 8.35 us: local(): lax.all_to_all(outgoing.reshape(devices, capacity, share), 'dp', split_ax...]
  transfers between devices with their start and end apart: 6 -> 18, of which waited for: 6 -> 9; matrix products, arithmetic and copies ran while one was open for 1% -> 5% of each run, Pallas kernels for 0% -> 28%
where the time goes in v1:
time: 121 us
  Pallas kernels  47.8 us (40%)
  waiting for transfers between devices  39.2 us (32%)
  starting transfers between devices  21.6 us (18%)
  other arithmetic  4.41 us (4%)
  local copies, waits for them, and re-layouts  3.91 us (3%)
  matrix products  3.55 us (3%)
    ppermute x18, waiting for transfers between devices, move(): return lax.ppermute(value, AXES, pairs)  39.2 us
    pallas_call x4, Pallas kernels, group_part(): pl.pallas_call(lambda *refs: group_kernel(*refs, peer=peer, chips=chips,...  24.3 us
    ppermute x18, starting transfers between devices, move(): return lax.ppermute(value, AXES, pairs)  21.6 us
    pallas_call x1, Pallas kernels, precond_part(): pl.pallas_call(lambda *refs: precond_kernel(*refs, cut=cut, blocks=blocks...  13.8 us
    pallas_call x1, Pallas kernels, near_part(): pl.pallas_call(lambda *refs: near_kernel(*refs, chips=chips, lanes=lanes,...  9.79 us
    dot_general x1, matrix products, contract(): lax.dot_general(left, right, (((1,), (1,)), ((), ())), preferred_element_...  2.67 us
  transfers between devices with their start and end apart: 18, of which 9 were waited for; matrix products, arithmetic and copies ran while one was open for 5% of the time, Pallas kernels for 28%

profile of v1, /device:TPU:0, one launch (start us, length us, event | category | flops | bytes accessed | tf_op | source)
XLA Modules:
  0.0 120.7 jit_solution(4219055482483246718)
XLA Ops:
  0.7 13.8 %shard_map.68 = (f32[256,1024]{1,0:T(8,128)}, f32[1,256,1024]{2,1,0:T(8,128)}) custom-call(s32[3]{0:T(128)} %pad_add_fusion.refs_0_, bf16[512,8192]{1,0:T(8,128)(2,1)} %refs_1_.9, bf16[8192,1024]{1,0:T(8,128)(2,1)} %refs_2_.1), custom_call_target="tpu_custom_call" | custom-call | flops 8589934592 | bytes 25165824 | tf_op jit(solution)/shard_map/pallas_call | solution.py:57
  16.4 6.0 %shard_map.66 = bf16[144,2048]{1,0:T(8,128)(2,1)} custom-call(s32[3]{0:T(128)} %pad_add_fusion.refs_0_, bf16[1024,8192]{1,0:T(8,128)(2,1)} %refs_1_.8, f32[8,8,1024]{2,1,0:T(8,128)} %bitcast.32, bf16[128,1024]{1,0:T(8,128)(2,1)} %fusion.3.refs_3_, bf16[16,128]{1,0:T(8,128)(2,1)} %fusion.21.refs_4_), custom_call_target="tpu_custom_call" | custom-call | flops 536870912 | bytes 4194304 | tf_op jit(solution)/shard_map/pallas_call | solution.py:122
  22.4 2.6 %collective-permute-start.1 = (bf16[144,2048]{1,0:T(8,128)(2,1)}, bf16[144,2048]{1,0:T(8,128)(2,1)S(1)}, u32[]{:S(2)}, u32[]{:S(2)}) collective-permute-start(bf16[144,2048]{1,0:T(8,128)(2,1)} %shard_map.66), channel_id=1, source_target_pairs={{0,4},{1,5},{2,6},{3,7},{4,0},{5,1},{6,2},{7,3},{8,12},{9,13},{10,... | collective-permute-start | bytes 1769480 | tf_op jit(solution)/shard_map/ppermute | solution.py:263
  25.0 6.0 %shard_map.65 = bf16[144,2048]{1,0:T(8,128)(2,1)} custom-call(s32[3]{0:T(128)} %pad_add_fusion.refs_0_, bf16[1024,8192]{1,0:T(8,128)(2,1)} %refs_1_.8, f32[8,8,1024]{2,1,0:T(8,128)} %bitcast.33, bf16[128,1024]{1,0:T(8,128)(2,1)} %fusion.3.refs_3_, bf16[16,128]{1,0:T(8,128)(2,1)} %fusion.21.refs_4_), custom_call_target="tpu_custom_call" | custom-call | flops 536870912 | bytes 4194304 | tf_op jit(solution)/shard_map/pallas_call | solution.py:122
  31.0 1.6 %collective-permute-start = (bf16[144,2048]{1,0:T(8,128)(2,1)}, bf16[144,2048]{1,0:T(8,128)(2,1)}, u32[]{:S(2)}, u32[]{:S(2)}) collective-permute-start(bf16[144,2048]{1,0:T(8,128)(2,1)} %shard_map.65), channel_id=1, source_target_pairs={{0,2},{1,3},{2,0},{3,1},{4,6},{5,7},{6,4},{7,5},{8,10},{9,11},{10,... | collective-permute-start | bytes 1769480 | tf_op jit(solution)/shard_map/ppermute | solution.py:263
  32.6 6.0 %shard_map.67 = bf16[144,2048]{1,0:T(8,128)(2,1)} custom-call(s32[3]{0:T(128)} %pad_add_fusion.refs_0_, bf16[1024,8192]{1,0:T(8,128)(2,1)} %refs_1_.8, f32[8,8,1024]{2,1,0:T(8,128)} %bitcast.34, bf16[128,1024]{1,0:T(8,128)(2,1)} %fusion.3.refs_3_, bf16[16,128]{1,0:T(8,128)(2,1)} %fusion.21.refs_4_), custom_call_target="tpu_custom_call" | custom-call | flops 536870912 | bytes 4194304 | tf_op jit(solution)/shard_map/pallas_call | solution.py:122
  38.7 6.2 %shard_map.64.refs_2_ = bf16[144,2048]{1,0:T(8,128)(2,1)} custom-call(s32[3]{0:T(128)} %pad_add_fusion.refs_0_, bf16[1024,8192]{1,0:T(8,128)(2,1)} %refs_1_.8, f32[8,8,1024]{2,1,0:T(8,128)} %bitcast.35, bf16[128,1024]{1,0:T(8,128)(2,1)} %fusion.3.refs_3_, bf16[16,128]{1,0:T(8,128)(2,1)} %fusion.21.refs_4_), custom_call_target="tpu_custom_call" | custom-call | flops 536870912 | bytes 4194304 | tf_op jit(solution)/shard_map/pallas_call | solution.py:122
  48.5 2.7 %collective-permute-start.9 = (bf16[256,1024]{1,0:T(8,128)(2,1)S(1)}, bf16[256,1024]{1,0:T(8,128)(2,1)S(1)}, u32[]{:S(2)}, u32[]{:S(2)}) collective-permute-start(bf16[256,1024]{1,0:T(8,128)(2,1)S(1)} %add_convert_fusion.1.refs_10_), channel_id=1, source_target_pairs={{0,16},{1,17},{2,18},{3,19},{4,20},{5,21},{6,22},{7,23},{8,24},{9,... | collective-permute-start | bytes 1572872 | tf_op jit(solution)/shard_map/ppermute | solution.py:263
  51.1 8.1 %collective-permute-done.2.refs_5_ = bf16[144,2048]{1,0:T(8,128)(2,1)} collective-permute-done((bf16[144,2048]{1,0:T(8,128)(2,1)}, bf16[144,2048]{1,0:T(8,128)(2,1)}, u32[]{:S(2)}, u32[]{:S(2)}) %collective-permute-start.2) | collective-permute-done | bytes 589856 | tf_op jit(solution)/shard_map/ppermute | solution.py:263
  60.2 1.9 %collective-permute-start.8 = (bf16[256,1024]{1,0:T(8,128)(2,1)S(1)}, bf16[256,1024]{1,0:T(8,128)(2,1)S(1)}, u32[]{:S(2)}, u32[]{:S(2)}) collective-permute-start(bf16[256,1024]{1,0:T(8,128)(2,1)S(1)} %add_convert_fusion.1.refs_10_), channel_id=1, source_target_pairs={{0,8},{1,9},{2,10},{3,11},{4,12},{5,13},{6,14},{7,15},{8,0},{9,1},... | collective-permute-start | bytes 1572872 | tf_op jit(solution)/shard_map/ppermute | solution.py:263
  62.1 1.5 %collective-permute-start.10 = (bf16[256,1024]{1,0:T(8,128)(2,1)S(1)}, bf16[256,1024]{1,0:T(8,128)(2,1)}, u32[]{:S(2)}, u32[]{:S(2)}) collective-permute-start(bf16[256,1024]{1,0:T(8,128)(2,1)S(1)} %add_convert_fusion.1.refs_10_), channel_id=1, source_target_pairs={{8,16},{9,17},{10,18},{11,19},{12,20},{13,21},{14,22},{15,23},{16,... | collective-permute-start | bytes 1572872 | tf_op jit(solution)/shard_map/ppermute | solution.py:263
  63.5 12.0 %collective-permute-done.9.refs_12_ = bf16[256,1024]{1,0:T(8,128)(2,1)S(1)} collective-permute-done((bf16[256,1024]{1,0:T(8,128)(2,1)S(1)}, bf16[256,1024]{1,0:T(8,128)(2,1)S(1)}, u32[]{:S(2)}, u32[]{:S(2)}) %collective-permute-start.9) | collective-permute-done | bytes 524320 | tf_op jit(solution)/shard_map/ppermute | solution.py:263
  75.5 1.3 %collective-permute-start.11 = (bf16[256,1024]{1,0:T(8,128)(2,1)S(1)}, bf16[256,1024]{1,0:T(8,128)(2,1)}, u32[]{:S(2)}, u32[]{:S(2)}) collective-permute-start(bf16[256,1024]{1,0:T(8,128)(2,1)S(1)} %collective-permute-done.9.refs_12_), channel_id=1, source_target_pairs={{8,0},{9,1},{10,2},{11,3},{12,4},{13,5},{14,6},{15,7},{16,24},{17,... | collective-permute-start | bytes 1572872 | tf_op jit(solution)/shard_map/ppermute | solution.py:263
  77.1 1.4 %fusion.refs_1_ = bf16[1024,512]{1,0:T(8,128)(2,1)} fusion(s32[512]{0:T(512)S(1)} %fusion.25), kind=kLoop, calls=%fused_computation.1 | loop fusion | flops 1048576 | bytes 1050624 | tf_op jit(solution)/shard_map/convert_element_type | solution.py:320
  79.4 5.8 %collective-permute-done.8.refs_11_ = bf16[256,1024]{1,0:T(8,128)(2,1)S(1)} collective-permute-done((bf16[256,1024]{1,0:T(8,128)(2,1)S(1)}, bf16[256,1024]{1,0:T(8,128)(2,1)S(1)}, u32[]{:S(2)}, u32[]{:S(2)}) %collective-permute-start.8) | collective-permute-done | bytes 524320 | tf_op jit(solution)/shard_map/ppermute | solution.py:263
  86.0 9.8 %near.1 = (f32[1024,256]{1,0:T(8,128)}, bf16[1024,1024]{1,0:T(8,128)(2,1)}) custom-call(s32[3]{0:T(128)} %pad_add_fusion.refs_0_, bf16[1024,512]{1,0:T(8,128)(2,1)} %fusion.refs_1_, bf16[144,2048]{1,0:T(8,128)(2,1)} %shard_map.64.refs_2_, bf16[144,2048]{1,0:T(8,128)(2,1)} %collective-permute-done.refs_3_, bf16[144,2048]{1,0:T(8,128)(2,1)} %copy-done.3, ...), custom_call_target="tpu_custom_call" | custom-call | flops 805306368 | bytes 8388608 | tf_op jit(solution)/shard_map/near/pallas_call | solution.py:207
  96.1 2.7 %fusion.1 = f32[1024,256]{1,0:T(8,128)S(1)} fusion(bf16[1024,1024]{1,0:T(8,128)(2,1)} %get-tuple-element.12, bf16[256,1024]{1,0:T(8,128)(2,1)} %collective-permute-done.10, bf16[256,1024]{1,0:T(8,128)(2,1)} %collective-permute-done.11), kind=kOutput, calls=%fused_computation.5 | convolution fusion | flops 537133056 | bytes 4194304 | tf_op jit(solution)/shard_map/dot_general | solution.py:355
  99.0 1.7 %collective-permute-start.12 = (bf16[256,256]{1,0:T(8,128)(2,1)S(1)}, bf16[256,256]{1,0:T(8,128)(2,1)S(1)}, u32[]{:S(2)}, u32[]{:S(2)}) collective-permute-start(bf16[256,256]{1,0:T(8,128)(2,1)S(1)} %get-tuple-element.13), channel_id=1, source_target_pairs={{0,2},{1,3},{2,0},{3,1},{4,6},{5,7},{6,4},{7,5},{8,10},{9,11},{10,... | collective-permute-start | bytes 393224 | tf_op jit(solution)/shard_map/ppermute | solution.py:263
  100.7 1.5 %collective-permute-start.13 = (bf16[256,256]{1,0:T(8,128)(2,1)S(1)}, bf16[256,256]{1,0:T(8,128)(2,1)S(1)}, u32[]{:S(2)}, u32[]{:S(2)}) collective-permute-start(bf16[256,256]{1,0:T(8,128)(2,1)S(1)} %get-tuple-element.15), channel_id=1, source_target_pairs={{0,4},{1,5},{2,6},{3,7},{4,0},{5,1},{6,2},{7,3},{8,12},{9,13},{10,... | collective-permute-start | bytes 393224 | tf_op jit(solution)/shard_map/ppermute | solution.py:263
  102.7 2.0 %collective-permute-done.12 = bf16[256,256]{1,0:T(8,128)(2,1)S(1)} collective-permute-done((bf16[256,256]{1,0:T(8,128)(2,1)S(1)}, bf16[256,256]{1,0:T(8,128)(2,1)S(1)}, u32[]{:S(2)}, u32[]{:S(2)}) %collective-permute-start.12) | collective-permute-done | bytes 131104 | tf_op jit(solution)/shard_map/ppermute | solution.py:263
  104.6 3.9 %collective-permute-done.13 = bf16[256,256]{1,0:T(8,128)(2,1)S(1)} collective-permute-done((bf16[256,256]{1,0:T(8,128)(2,1)S(1)}, bf16[256,256]{1,0:T(8,128)(2,1)S(1)}, u32[]{:S(2)}, u32[]{:S(2)}) %collective-permute-start.13) | collective-permute-done | bytes 131104 | tf_op jit(solution)/shard_map/ppermute | solution.py:263
  108.8 5.1 %collective-permute-start.16 = (bf16[64,384]{1,0:T(8,128)(2,1)S(1)}, bf16[64,384]{1,0:T(8,128)(2,1)S(1)}, u32[]{:S(2)}, u32[]{:S(2)}) collective-permute-start(bf16[64,384]{1,0:T(8,128)(2,1)S(1)} %bitcast.39), channel_id=1, source_target_pairs={{0,16},{1,17},{2,18},{3,19},{4,20},{5,21},{6,22},{7,23},{8,24},{9,... | collective-permute-start | bytes 147464 | tf_op jit(solution)/shard_map/ppermute | solution.py:263
  114.0 3.1 %collective-permute-done.16 = bf16[64,384]{1,0:T(8,128)(2,1)S(1)} collective-permute-done((bf16[64,384]{1,0:T(8,128)(2,1)S(1)}, bf16[64,384]{1,0:T(8,128)(2,1)S(1)}, u32[]{:S(2)}, u32[]{:S(2)}) %collective-permute-start.16) | collective-permute-done | bytes 49184 | tf_op jit(solution)/shard_map/ppermute | solution.py:263
  117.0 2.8 %collective-permute-done.17 = bf16[64,384]{1,0:T(8,128)(2,1)S(1)} collective-permute-done((bf16[64,384]{1,0:T(8,128)(2,1)S(1)}, bf16[64,384]{1,0:T(8,128)(2,1)S(1)}, u32[]{:S(2)}, u32[]{:S(2)}) %collective-permute-start.17) | collective-permute-done | bytes 49184 | tf_op jit(solution)/shard_map/ppermute | solution.py:263
  (67 shorter events, 11.2 us)
Async XLA Ops:
  0.7 14.3 %copy-start.10 = (s32[128]{0:T(128)S(1)}, s32[128]{0:T(128)}, u32[]{:S(2)}) copy-start(s32[128]{0:T(128)} %param.9) | copy-start | bytes 1540
  0.7 14.3 %copy-start.9 = (s32[1,1024]{1,0:T(1,128)S(1)}, s32[1,1024]{1,0:T(1,128)}, u32[]{:S(2)}) copy-start(s32[1,1024]{1,0:T(1,128)} %param.8) | copy-start | bytes 12292
  14.4 33.8 %collective-permute-start.7 = (f32[256,1024]{1,0:T(8,128)}, f32[256,1024]{1,0:T(8,128)S(1)}, u32[]{:S(2)}, u32[]{:S(2)}) collective-permute-start(f32[256,1024]{1,0:T(8,128)} %bitcast.46), channel_id=1, source_target_pairs={{0,1},{1,0},{2,3},{3,2},{4,5},{5,4},{6,7},{7,6},{8,9},{9,8},{10,11... | collective-permute-start | bytes 3145736 | tf_op jit(solution)/shard_map/ppermute | solution.py:263
  22.4 23.5 %collective-permute-start.1 = (bf16[144,2048]{1,0:T(8,128)(2,1)}, bf16[144,2048]{1,0:T(8,128)(2,1)S(1)}, u32[]{:S(2)}, u32[]{:S(2)}) collective-permute-start(bf16[144,2048]{1,0:T(8,128)(2,1)} %shard_map.66), channel_id=1, source_target_pairs={{0,4},{1,5},{2,6},{3,7},{4,0},{5,1},{6,2},{7,3},{8,12},{9,13},{10,... | collective-permute-start | bytes 1769480 | tf_op jit(solution)/shard_map/ppermute | solution.py:263
  31.0 16.6 %collective-permute-start = (bf16[144,2048]{1,0:T(8,128)(2,1)}, bf16[144,2048]{1,0:T(8,128)(2,1)}, u32[]{:S(2)}, u32[]{:S(2)}) collective-permute-start(bf16[144,2048]{1,0:T(8,128)(2,1)} %shard_map.65), channel_id=1, source_target_pairs={{0,2},{1,3},{2,0},{3,1},{4,6},{5,7},{6,4},{7,5},{8,10},{9,11},{10,... | collective-permute-start | bytes 1769480 | tf_op jit(solution)/shard_map/ppermute | solution.py:263
  38.7 20.6 %collective-permute-start.2 = (bf16[144,2048]{1,0:T(8,128)(2,1)}, bf16[144,2048]{1,0:T(8,128)(2,1)}, u32[]{:S(2)}, u32[]{:S(2)}) collective-permute-start(bf16[144,2048]{1,0:T(8,128)(2,1)} %shard_map.67), channel_id=1, source_target_pairs={{0,6},{1,7},{2,4},{3,5},{4,2},{5,3},{6,0},{7,1},{8,14},{9,15},{10,... | collective-permute-start | bytes 1769480 | tf_op jit(solution)/shard_map/ppermute | solution.py:263
  44.9 15.3 %collective-permute-start.3 = (bf16[144,2048]{1,0:T(8,128)(2,1)}, bf16[144,2048]{1,0:T(8,128)(2,1)}, u32[]{:S(2)}, u32[]{:S(2)}) collective-permute-start(bf16[144,2048]{1,0:T(8,128)(2,1)} %shard_map.64.refs_2_), channel_id=1, source_target_pairs={{0,1},{1,0},{2,3},{3,2},{4,5},{5,4},{6,7},{7,6},{8,9},{9,8},{10,11... | collective-permute-start | bytes 1769480 | tf_op jit(solution)/shard_map/ppermute | solution.py:263
  45.9 39.3 %copy-start.3 = (bf16[144,2048]{1,0:T(8,128)(2,1)}, bf16[144,2048]{1,0:T(8,128)(2,1)S(1)}, u32[]{:S(2)}) copy-start(bf16[144,2048]{1,0:T(8,128)(2,1)S(1)} %collective-permute-done.1.refs_4_) | copy-start | bytes 1769476
  45.9 32.6 %collective-permute-start.5 = (bf16[144,2048]{1,0:T(8,128)(2,1)S(1)}, bf16[144,2048]{1,0:T(8,128)(2,1)S(1)}, u32[]{:S(2)}, u32[]{:S(2)}) collective-permute-start(bf16[144,2048]{1,0:T(8,128)(2,1)S(1)} %collective-permute-done.1.refs_4_), channel_id=1, source_target_pairs={{0,1},{1,0},{2,3},{3,2},{4,5},{5,4},{6,7},{7,6},{8,9},{9,8},{10,11... | collective-permute-start | bytes 1769480 | tf_op jit(solution)/shard_map/ppermute | solution.py:263
  47.6 14.4 %collective-permute-start.4 = (bf16[144,2048]{1,0:T(8,128)(2,1)}, bf16[144,2048]{1,0:T(8,128)(2,1)S(1)}, u32[]{:S(2)}, u32[]{:S(2)}) collective-permute-start(bf16[144,2048]{1,0:T(8,128)(2,1)} %collective-permute-done.refs_3_), channel_id=1, source_target_pairs={{0,1},{1,0},{2,3},{3,2},{4,5},{5,4},{6,7},{7,6},{8,9},{9,8},{10,11... | collective-permute-start | bytes 1769480 | tf_op jit(solution)/shard_map/ppermute | solution.py:263
  48.5 36.7 %copy-start = (bf16[256,1024]{1,0:T(8,128)(2,1)}, bf16[256,1024]{1,0:T(8,128)(2,1)S(1)}, u32[]{:S(2)}) copy-start(bf16[256,1024]{1,0:T(8,128)(2,1)S(1)} %add_convert_fusion.1.refs_10_) | copy-start | bytes 1572868
  48.5 27.0 %collective-permute-start.9 = (bf16[256,1024]{1,0:T(8,128)(2,1)S(1)}, bf16[256,1024]{1,0:T(8,128)(2,1)S(1)}, u32[]{:S(2)}, u32[]{:S(2)}) collective-permute-start(bf16[256,1024]{1,0:T(8,128)(2,1)S(1)} %add_convert_fusion.1.refs_10_), channel_id=1, source_target_pairs={{0,16},{1,17},{2,18},{3,19},{4,20},{5,21},{6,22},{7,23},{8,24},{9,... | collective-permute-start | bytes 1572872 | tf_op jit(solution)/shard_map/ppermute | solution.py:263
  59.9 19.4 %collective-permute-start.6 = (bf16[144,2048]{1,0:T(8,128)(2,1)}, bf16[144,2048]{1,0:T(8,128)(2,1)S(1)}, u32[]{:S(2)}, u32[]{:S(2)}) collective-permute-start(bf16[144,2048]{1,0:T(8,128)(2,1)} %collective-permute-done.2.refs_5_), channel_id=1, source_target_pairs={{0,1},{1,0},{2,3},{3,2},{4,5},{5,4},{6,7},{7,6},{8,9},{9,8},{10,11... | collective-permute-start | bytes 1769480 | tf_op jit(solution)/shard_map/ppermute | solution.py:263
  60.2 25.0 %collective-permute-start.8 = (bf16[256,1024]{1,0:T(8,128)(2,1)S(1)}, bf16[256,1024]{1,0:T(8,128)(2,1)S(1)}, u32[]{:S(2)}, u32[]{:S(2)}) collective-permute-start(bf16[256,1024]{1,0:T(8,128)(2,1)S(1)} %add_convert_fusion.1.refs_10_), channel_id=1, source_target_pairs={{0,8},{1,9},{2,10},{3,11},{4,12},{5,13},{6,14},{7,15},{8,0},{9,1},... | collective-permute-start | bytes 1572872 | tf_op jit(solution)/shard_map/ppermute | solution.py:263
  62.1 17.3 %copy-start.5 = (bf16[144,2048]{1,0:T(8,128)(2,1)}, bf16[144,2048]{1,0:T(8,128)(2,1)S(1)}, u32[]{:S(2)}) copy-start(bf16[144,2048]{1,0:T(8,128)(2,1)S(1)} %collective-permute-done.4.refs_7_) | copy-start | bytes 1769476
  62.1 33.7 %collective-permute-start.10 = (bf16[256,1024]{1,0:T(8,128)(2,1)S(1)}, bf16[256,1024]{1,0:T(8,128)(2,1)}, u32[]{:S(2)}, u32[]{:S(2)}) collective-permute-start(bf16[256,1024]{1,0:T(8,128)(2,1)S(1)} %add_convert_fusion.1.refs_10_), channel_id=1, source_target_pairs={{8,16},{9,17},{10,18},{11,19},{12,20},{13,21},{14,22},{15,23},{16,... | collective-permute-start | bytes 1572872 | tf_op jit(solution)/shard_map/ppermute | solution.py:263
  75.5 9.7 %copy-start.7 = (bf16[256,1024]{1,0:T(8,128)(2,1)}, bf16[256,1024]{1,0:T(8,128)(2,1)S(1)}, u32[]{:S(2)}) copy-start(bf16[256,1024]{1,0:T(8,128)(2,1)S(1)} %collective-permute-done.9.refs_12_) | copy-start | bytes 1572868
  75.5 20.6 %collective-permute-start.11 = (bf16[256,1024]{1,0:T(8,128)(2,1)S(1)}, bf16[256,1024]{1,0:T(8,128)(2,1)}, u32[]{:S(2)}, u32[]{:S(2)}) collective-permute-start(bf16[256,1024]{1,0:T(8,128)(2,1)S(1)} %collective-permute-done.9.refs_12_), channel_id=1, source_target_pairs={{8,0},{9,1},{10,2},{11,3},{12,4},{13,5},{14,6},{15,7},{16,24},{17,... | collective-permute-start | bytes 1572872 | tf_op jit(solution)/shard_map/ppermute | solution.py:263
  99.0 5.6 %collective-permute-start.12 = (bf16[256,256]{1,0:T(8,128)(2,1)S(1)}, bf16[256,256]{1,0:T(8,128)(2,1)S(1)}, u32[]{:S(2)}, u32[]{:S(2)}) collective-permute-start(bf16[256,256]{1,0:T(8,128)(2,1)S(1)} %get-tuple-element.13), channel_id=1, source_target_pairs={{0,2},{1,3},{2,0},{3,1},{4,6},{5,7},{6,4},{7,5},{8,10},{9,11},{10,... | collective-permute-start | bytes 393224 | tf_op jit(solution)/shard_map/ppermute | solution.py:263
  100.7 7.8 %collective-permute-start.13 = (bf16[256,256]{1,0:T(8,128)(2,1)S(1)}, bf16[256,256]{1,0:T(8,128)(2,1)S(1)}, u32[]{:S(2)}, u32[]{:S(2)}) collective-permute-start(bf16[256,256]{1,0:T(8,128)(2,1)S(1)} %get-tuple-element.15), channel_id=1, source_target_pairs={{0,4},{1,5},{2,6},{3,7},{4,0},{5,1},{6,2},{7,3},{8,12},{9,13},{10,... | collective-permute-start | bytes 393224 | tf_op jit(solution)/shard_map/ppermute | solution.py:263
  102.2 6.3 %collective-permute-start.14 = (bf16[256,256]{1,0:T(8,128)(2,1)S(1)}, bf16[256,256]{1,0:T(8,128)(2,1)S(1)}, u32[]{:S(2)}, u32[]{:S(2)}) collective-permute-start(bf16[256,256]{1,0:T(8,128)(2,1)S(1)} %get-tuple-element.14), channel_id=1, source_target_pairs={{0,6},{1,7},{2,4},{3,5},{4,2},{5,3},{6,0},{7,1},{8,14},{9,15},{10,... | collective-permute-start | bytes 393224 | tf_op jit(solution)/shard_map/ppermute | solution.py:263
  108.7 5.2 %collective-permute-start.15 = (bf16[64,384]{1,0:T(8,128)(2,1)S(1)}, bf16[64,384]{1,0:T(8,128)(2,1)S(1)}, u32[]{:S(2)}, u32[]{:S(2)}) collective-permute-start(bf16[64,384]{1,0:T(8,128)(2,1)S(1)} %bitcast.40), channel_id=1, source_target_pairs={{0,8},{1,9},{2,10},{3,11},{4,12},{5,13},{6,14},{7,15},{8,0},{9,1},... | collective-permute-start | bytes 147464 | tf_op jit(solution)/shard_map/ppermute | solution.py:263
  108.8 8.2 %collective-permute-start.16 = (bf16[64,384]{1,0:T(8,128)(2,1)S(1)}, bf16[64,384]{1,0:T(8,128)(2,1)S(1)}, u32[]{:S(2)}, u32[]{:S(2)}) collective-permute-start(bf16[64,384]{1,0:T(8,128)(2,1)S(1)} %bitcast.39), channel_id=1, source_target_pairs={{0,16},{1,17},{2,18},{3,19},{4,20},{5,21},{6,22},{7,23},{8,24},{9,... | collective-permute-start | bytes 147464 | tf_op jit(solution)/shard_map/ppermute | solution.py:263
  113.9 5.9 %collective-permute-start.17 = (bf16[64,384]{1,0:T(8,128)(2,1)S(1)}, bf16[64,384]{1,0:T(8,128)(2,1)S(1)}, u32[]{:S(2)}, u32[]{:S(2)}) collective-permute-start(bf16[64,384]{1,0:T(8,128)(2,1)S(1)} %bitcast.38), channel_id=1, source_target_pairs={{0,24},{1,25},{2,26},{3,27},{4,28},{5,29},{6,30},{7,31},{8,16},{9,... | collective-permute-start | bytes 147464 | tf_op jit(solution)/shard_map/ppermute | solution.py:263
  (5 other events, 19.8 us)

commit v2 on v0

v2 whole, which is shorter than its diff:
```python
import jax
import jax.numpy as jnp
from jax import lax
from jax.experimental import pallas as pl
from jax.experimental.pallas import tpu as pltpu
from jax.sharding import PartitionSpec as P

QBLOCK = 128
GRP_DEV = 128
AXES = ("dp", "mp")
LANES = 128


ANYWHERE = pl.BlockSpec(memory_space=pl.ANY)
ON_CHIP = pl.BlockSpec(memory_space=pltpu.VMEM)


def room(*sizes):
    return pltpu.CompilerParams(vmem_limit_bytes=sum(sizes) + (4 << 20))


def on_chip(value):
    return pltpu.with_memory_space_constraint(value, pltpu.VMEM)


def precond_kernel(queries, inv_hess, mine, *refs, cut, blocks):
    theirs, (left, right, acc, sems) = refs[:-4], refs[-4:]
    width = right.shape[1]
    copies = []
    start = 0
    for i, depth in enumerate(blocks):
        span = pl.ds(start, depth)
        pair = (
            pltpu.make_async_copy(queries.at[:, span], left.at[:, span], sems.at[0, i]),
            pltpu.make_async_copy(
                inv_hess.at[span, pl.ds(cut * width, width)], right.at[span, :], sems.at[1, i]
            ),
        )
        for copy in pair:
            copy.start()
        copies.append((span, pair))
        start += depth
    for i, (span, pair) in enumerate(copies):
        for copy in pair:
            copy.wait()
        product = jnp.dot(left[:, span], right[span, :], preferred_element_type=jnp.float32)
        if i == 0:
            acc[...] = product
        else:
            acc[...] += product
    lane, share = lax.axis_index("mp"), mine.shape[0]
    mine[...] = acc[pl.ds(lane * share, share), :]
    for other, out in enumerate(theirs):
        first = jnp.bitwise_xor(lane, other + 1) * share
        out[...] = acc[pl.ds(first, share), :]


def precond_part(queries, inv_hess, lanes, cut, cuts):
    count, depth = queries.shape
    width = inv_hess.shape[1] // cuts
    share = count // lanes
    unit = depth // 16
    blocks = (unit, unit, 2 * unit, 4 * unit, 4 * unit, 4 * unit)
    return pl.pallas_call(
        lambda *refs: precond_kernel(*refs, cut=cut, blocks=blocks),
        in_specs=[ANYWHERE, ANYWHERE],
        out_specs=[ON_CHIP] * lanes,
        scratch_shapes=[
            pltpu.VMEM((count, depth), queries.dtype),
            pltpu.VMEM((depth, width), inv_hess.dtype),
            pltpu.VMEM((count, width), jnp.float32),
            pltpu.SemaphoreType.DMA((2, len(blocks))),
        ],
        out_shape=[pltpu.VMEM((share, width), jnp.float32)] * lanes,
        cost_estimate=pl.CostEstimate(
            flops=2 * count * depth * width,
            transcendentals=0,
            bytes_accessed=2 * (count * depth + depth * width),
        ),
        name="precond",
    )(queries, inv_hess)


def group_kernel(grads, scales, onehot, *refs, peers, chips, columns, width):
    outs, buffer, sems = refs[:-2], refs[-2], refs[-1]
    rows = buffer.shape[1]
    blocks = width // QBLOCK
    copies = []
    for out, peer in zip(outs, peers):
        for c in range(columns):
            column = c * chips + jnp.bitwise_xor(lax.axis_index("dp") % chips, peer)
            copy = pltpu.make_async_copy(
                grads.at[:, pl.ds(pl.multiple_of(column * width, width), width)],
                buffer.at[len(copies)],
                sems.at[len(copies)],
            )
            copy.start()
            copies.append((copy, out, column, c * width))
    for i, (copy, out, column, at) in enumerate(copies):
        copy.wait()
        turned = buffer[i].T.astype(jnp.float32).reshape(blocks, QBLOCK, rows)
        dequant = (turned * scales[column][:, None, :]).astype(jnp.bfloat16).reshape(width, rows)
        out[:, at : at + width] = lax.dot_general(
            onehot[...], dequant, (((1,), (1,)), ((), ())), preferred_element_type=jnp.float32
        ).astype(jnp.bfloat16)


def group_part(grads, scales, onehot, peers, chips, columns, width):
    rows = grads.shape[0]
    groups = onehot.shape[0]
    scales = scales.reshape(-1, width // QBLOCK, rows)
    shape = (groups, columns * width)
    count = len(peers) * columns
    return pl.pallas_call(
        lambda *refs: group_kernel(
            *refs, peers=peers, chips=chips, columns=columns, width=width
        ),
        in_specs=[ANYWHERE, ON_CHIP, ON_CHIP],
        out_specs=[ON_CHIP for _ in peers],
        scratch_shapes=[
            pltpu.VMEM((count, rows, width), grads.dtype),
            pltpu.SemaphoreType.DMA((count,)),
        ],
        out_shape=[pltpu.VMEM(shape, jnp.bfloat16) for _ in peers],
        cost_estimate=pl.CostEstimate(
            flops=2 * groups * rows * count * width,
            transcendentals=0,
            bytes_accessed=2 * rows * count * width,
        ),
    )(grads, on_chip(scales), on_chip(onehot))


def hop_of(pair):
    at_end, between = pair
    if at_end == between:
        return at_end, True
    where = lax.axis_index("dp") // (lax.axis_size("dp") // 4)
    inside = (where == 1) | (where == 2)
    if at_end is None:
        return between, inside
    if between is None:
        return at_end, jnp.logical_not(inside)
    return jnp.where(inside, between, at_end), True


def when(condition):
    return (lambda body: body()) if condition is True else pl.when(condition)


def near_kernel(*refs, hops, late, chips, lanes, per_lane, plane):
    pieces, refs = refs[: chips * lanes], refs[chips * lanes :]
    precond, total, left = refs[: len(hops)], refs[len(hops)], refs[-1]
    fars = refs[len(hops) + 1 : -1]
    rows, width = left.shape
    groups = rows // chips
    at_line = lax.axis_index("dp") // plane

    def lay(target, hop):
        source = jnp.bitwise_xor(at_line, hop)
        holder = jnp.bitwise_xor(source // per_lane, lax.axis_index("mp"))
        inner = source % per_lane
        for lane in range(lanes):
            for k in range(per_lane):

                @pl.when((holder == lane) & (inner == k))
                def _():
                    for chip in range(chips):
                        target[chip * groups : (chip + 1) * groups, :] = pieces[
                            lane * chips + chip
                        ][:groups, k * width : (k + 1) * width]

    for i, (pair, block) in enumerate(zip(hops, precond)):
        hop, here = hop_of(pair)

        @when(here)
        def _():
            lay(left, hop)
            part = contract(left[...], block[...])
            total[...] = part if i == 0 else total[...] + part

    for pair, far in zip(late, fars):
        hop, here = hop_of(pair)
        when(here)(lambda: lay(far, hop))


def near_part(pieces, precond, hops, late, chips, lanes, per_lane, plane):
    share, width = precond[0].shape
    rows = chips * (pieces[0].shape[0])
    return pl.pallas_call(
        lambda *refs: near_kernel(
            *refs,
            hops=hops,
            late=late,
            chips=chips,
            lanes=lanes,
            per_lane=per_lane,
            plane=plane,
        ),
        in_specs=[ON_CHIP] * (len(pieces) + len(precond)),
        out_specs=[ON_CHIP] * (1 + len(late)),
        scratch_shapes=[pltpu.VMEM((rows, width), jnp.bfloat16)],
        out_shape=[
            pltpu.VMEM((rows, share), jnp.float32),
            *[pltpu.VMEM((rows, width), jnp.bfloat16) for _ in late],
        ],
        compiler_params=room(2 * rows * width, 16 * rows * share),
        cost_estimate=pl.CostEstimate(
            flops=2 * rows * width * share * len(hops),
            transcendentals=0,
            bytes_accessed=2 * rows * width * len(hops),
        ),
        name="near",
    )(*[on_chip(p) for p in pieces], *[on_chip(p) for p in precond])


def far_kernel(routing, *refs, late, chips, parts):
    totals, refs = refs[:parts], refs[parts:]
    fars, refs = refs[: parts * len(late)], refs[parts * len(late) :]
    blocks, outs, acc = refs[: len(late)], refs[len(late) : -1], refs[-1]
    start = 0
    for part, total in enumerate(totals):
        span = slice(start, start + total.shape[0])
        start += total.shape[0]
        for i, (pair, block) in enumerate(zip(late, blocks)):
            _, here = hop_of(pair)

            @when(here)
            def _():
                before = total[...] if i == 0 else acc[span, :]
                acc[span, :] = before + contract(fars[part * len(late) + i][...], block[...])

    sending = jnp.dot(
        routing[...], acc[...].astype(jnp.bfloat16), preferred_element_type=jnp.float32
    ).astype(jnp.bfloat16)
    rows = sending.shape[0] // chips
    for chip in range(chips):
        outs[chip][...] = sending[chip * rows : (chip + 1) * rows, :]


def far_part(totals, routing, fars, blocks, late, chips):
    share = totals[0].shape[1]
    rows = sum(t.shape[0] for t in totals)
    sent = routing.shape[0] // chips
    operands = (routing, *totals, *sum(fars, []), *blocks)
    return pl.pallas_call(
        lambda *refs: far_kernel(*refs, late=late, chips=chips, parts=len(totals)),
        in_specs=[ON_CHIP] * len(operands),
        out_specs=[ON_CHIP] * chips,
        scratch_shapes=[pltpu.VMEM((rows, share), jnp.float32)],
        out_shape=[pltpu.VMEM((sent, share), jnp.bfloat16)] * chips,
        compiler_params=room(8 * routing.shape[0] * share, 8 * rows * share),
        cost_estimate=pl.CostEstimate(
            flops=2 * rows * blocks[0].size,
            transcendentals=0,
            bytes_accessed=2 * rows * blocks[0].shape[1],
        ),
        name="far",
    )(*[on_chip(o) for o in operands])


def contract(left, right):
    return lax.dot_general(
        left, right, (((1,), (1,)), ((), ())), preferred_element_type=jnp.float32
    )


def local(grads, scales, example_group, group_slot, inv_hess, queries):
    devices = lax.axis_size("dp")
    lanes = lax.axis_size("mp")
    chips = 1 << ((devices.bit_length() - 1) // 2)
    line = devices // chips
    per_lane = line // lanes
    width = inv_hess.shape[1]
    share = queries.shape[0] // lanes
    capacity = 2 * GRP_DEV // devices
    at_line = lax.axis_index("dp") // chips
    at_plane = lax.axis_index("dp") % chips

    def move(value, target):
        pairs = []
        for s in range(line):
            for t in range(chips):
                for m in range(lanes):
                    to = target(s, t, m)
                    if to is not None:
                        a, b, c = to
                        pairs.append(((s * chips + t) * lanes + m, (a * chips + b) * lanes + c))
        return lax.ppermute(value, AXES, pairs)

    def to_lane(value, hop):
        return move(value, lambda s, t, m: (s, t, m ^ hop))

    def to_plane(value, hop):
        return move(value, lambda s, t, m: (s, t ^ hop, m))

    def to_line(value, hop):
        return move(value, lambda s, t, m: (s ^ hop, t, m))

    mine, *theirs = precond_part(queries, inv_hess, lanes, 0, 1)
    block = mine
    for hop in range(1, lanes):
        block = block + to_lane(theirs[hop - 1], hop)
    block = block.astype(jnp.bfloat16)
    if line == 4:
        inside = (at_line == 1) | (at_line == 2)
        outward = {0: 2, 3: 1, 2: 3, 1: 0}
        early = move(block, lambda s, t, m: (outward[s], t, m))
        skip = move(block, lambda s, t, m: (s ^ 2, t, m) if s in (1, 2) else None)
        middle = move(block, lambda s, t, m: (s ^ 3, t, m) if s in (1, 2) else None)
        onward = jnp.where(inside, early, block)
        relay = move(onward, lambda s, t, m: (s ^ 1, t, m))
        nearer = {(0, 0): block, (1, 2): early, (2, None): skip}
        later = {(3, 1): relay, (None, 3): middle}
    else:
        nearer = {(0, 0): block}
        for hop in range(1, line):
            nearer[hop, hop] = to_line(block, hop)
        later = {(line - 1, line - 1): nearer.pop((line - 1, line - 1))}

    slot = group_slot.reshape(1, GRP_DEV)
    slots = [slot] + [to_plane(slot, hop) for hop in range(1, chips)]
    onehot = (
        jnp.arange(GRP_DEV, dtype=jnp.int32)[:, None] == example_group[0][None, :]
    ).astype(jnp.bfloat16)
    pieces = [None] * chips
    for peers in ((chips - 1,), tuple(range(1, chips - 1)), (0,)):
        made = group_part(grads, scales, onehot, peers, chips, per_lane, width)
        for hop, piece in zip(peers, made):
            pieces[hop] = to_plane(piece, hop) if hop else piece
    held = list(pieces)
    for hop in range(1, lanes):
        held += [to_lane(piece, hop) for piece in pieces]

    halves = ((0, *range(chips - 1, chips // 2, -1)), tuple(range(1, chips // 2 + 1)))
    sequence = halves[0] + halves[1]
    slot = jnp.concatenate([slots[hop] for hop in sequence], axis=0)
    owner, inside_owner = slot // GRP_DEV, slot % GRP_DEV
    source = jnp.bitwise_xor(jnp.array(sequence, jnp.int32), at_plane)[:, None]
    order = jnp.arange(GRP_DEV, dtype=jnp.int32)
    earlier = (owner[:, :, None] == owner[:, None, :]) & (order[None, :] < order[:, None])[None]
    rank = jnp.sum(earlier.astype(jnp.int32), axis=2)
    per_chip = chips * line * capacity
    toward = jnp.bitwise_xor(owner % chips, at_plane)
    row = toward * per_chip + (source * line + owner // chips) * capacity + rank
    rows = jnp.arange(chips * per_chip, dtype=jnp.int32)[:, None]
    routing = (rows == row.reshape(1, -1)).astype(jnp.bfloat16)
    kept = rows[:per_chip] == row.reshape(1, -1)
    meta = GRP_DEV + jnp.sum(
        jnp.where(kept, inside_owner.reshape(1, -1) - GRP_DEV, 0), axis=1, keepdims=True
    )
    meta = jnp.broadcast_to(meta, (per_chip, LANES)).astype(jnp.bfloat16)
    meta = meta.reshape(chips, line, capacity, LANES)

    late = tuple(later)
    totals, fars = [], []
    for some in halves:
        total, *parts = near_part(
            [held[lane * chips + hop] for lane in range(lanes) for hop in some],
            list(nearer.values()),
            tuple(nearer),
            late,
            len(some),
            lanes,
            per_lane,
            chips,
        )
        totals.append(total)
        fars.append(parts)
    sending = far_part(totals, routing, fars, list(later.values()), late, chips)
    whole = sending[0].astype(jnp.float32)
    for hop in range(1, chips):
        whole = whole + to_plane(sending[hop], hop).astype(jnp.float32)
    whole = whole.astype(jnp.bfloat16).reshape(chips, line, capacity, share)
    whole = jnp.concatenate([whole, meta], axis=3)
    final = []
    for hop in range(line):
        own = lax.dynamic_index_in_dim(whole, jnp.bitwise_xor(at_line, hop), 1, keepdims=False)
        own = own.reshape(chips * capacity, share + LANES)
        final.append(to_line(own, hop) if hop else own)
    final = jnp.concatenate(final, axis=0)
    chosen = (final[:, share:] == jnp.arange(LANES, dtype=jnp.bfloat16)[None, :]).astype(
        jnp.bfloat16
    )
    return lax.dot_general(
        chosen, final[:, :share], (((0,), (0,)), ((), ())), preferred_element_type=jnp.float32
    )


def solution(mesh):
    in_specs = (P("dp", "mp"), P("mp", "dp"), P("dp", None), P("dp"), P("mp", "dp"), P(None, "mp"))
    out_specs = P("dp", "mp")

    return jax.shard_map(local, mesh=mesh, in_specs=in_specs, out_specs=out_specs, check_vma=False)
```

time: 409 us -> 101 us (0.25)
  waiting for transfers between devices: 296 us -> 33.3 us
  matrix products: 43.5 us -> 0.88 us
  local copies, waits for them, and re-layouts: 39.6 us -> 0.2 us
  Pallas kernels: 0 us -> 32.8 us
  starting transfers between devices: 8.22 us -> 31 us
  between operations: 13.2 us -> 0.23 us
  other arithmetic: 8.81 us -> 2.55 us
    psum x1 -> x0, waiting for transfers between devices: 259 us -> none  [spread_2(): return lax.psum(kept, axis)]
    dot_general x2 -> x1, matrix products: 43.5 us -> 0.88 us  [local(): lax.dot_general(chosen, final[:, :share], (((0,), (0,)), ((), ())), prefe...]
    ppermute x0 -> x21, waiting for transfers between devices: none -> 33.3 us  [move(): return lax.ppermute(value, AXES, pairs)]
    pallas_call x0 -> x7, Pallas kernels: none -> 32.8 us  [the longest x3 13.8 us: group_part(): pl.pallas_call(lambda *refs: group_kernel(*refs, peers=peers, chips=chips...]
    ppermute x0 -> x21, starting transfers between devices: none -> 31 us  [move(): return lax.ppermute(value, AXES, pairs)]
    mul x1 -> x0, local copies, waits for them, and re-layouts: 21.3 us -> none  [local(): grads.reshape(ex_rows, width // QBLOCK, QBLOCK)]
    all_to_all x2 -> x0, waiting for transfers between devices: 13.2 us -> none  [the longest x1 8.35 us: local(): lax.all_to_all(outgoing.reshape(devices, capacity, share), 'dp', split_ax...]
    reduce_scatter x2 -> x0, waiting for transfers between devices: 12.9 us -> none  [the longest x1 12.6 us: local(): lax.psum_scatter(jnp.dot(queries, inv_hess, preferred_element_type=jnp.fl...]
  transfers between devices with their start and end apart: 6 -> 21, of which waited for: 6 -> 7; matrix products, arithmetic and copies ran while one was open for 1% -> 3% of each run, Pallas kernels for 0% -> 19%
where the time goes in v2:
time: 101 us
  waiting for transfers between devices  33.3 us (33%)
  Pallas kernels  32.8 us (32%)
  starting transfers between devices  31 us (31%)
  other arithmetic  2.55 us (3%)
    ppermute x21, waiting for transfers between devices, move(): return lax.ppermute(value, AXES, pairs)  33.3 us
    ppermute x21, starting transfers between devices, move(): return lax.ppermute(value, AXES, pairs)  31 us
    pallas_call x3, Pallas kernels, group_part(): pl.pallas_call(lambda *refs: group_kernel(*refs, peers=peers, chips=chips...  13.8 us
    pallas_call x1, Pallas kernels, precond_part(): pl.pallas_call(lambda *refs: precond_kernel(*refs, cut=cut, blocks=blocks...  12.8 us
    pallas_call x2, Pallas kernels, near_part(): pl.pallas_call(lambda *refs: near_kernel(*refs, hops=hops, late=late, chi...  5.12 us
  transfers between devices with their start and end apart: 21, of which 7 were waited for; matrix products, arithmetic and copies ran while one was open for 3% of the time, Pallas kernels for 19%

profile of v2, /device:TPU:0, one launch (start us, length us, event | category | flops | bytes accessed | tf_op | source)
XLA Modules:
  0.0 101.0 jit_solution(15902997138367057591)
XLA Ops:
  0.0 12.8 %precond.1 = (f32[256,1024]{1,0:T(8,128)S(1)}, f32[256,1024]{1,0:T(8,128)}) custom-call(bf16[512,8192]{1,0:T(8,128)(2,1)} %refs_0_.6, bf16[8192,1024]{1,0:T(8,128)(2,1)} %refs_1_.1), custom_call_target="tpu_custom_call" | custom-call | flops 8589934592 | bytes 25165824 | tf_op jit(solution)/shard_map/precond/pallas_call | solution.py:64
  13.4 2.6 %collective-permute-start.2 = (s32[1,128]{1,0:T(1,128)S(1)}, s32[1,128]{1,0:T(1,128)S(1)}, u32[]{:S(2)}, u32[]{:S(2)}) collective-permute-start(s32[1,128]{1,0:T(1,128)S(1)} %bitcast.46), channel_id=1, source_target_pairs={{0,4},{1,5},{2,6},{3,7},{4,0},{5,1},{6,2},{7,3},{8,12},{9,13},{10,... | collective-permute-start | bytes 1544 | tf_op jit(solution)/shard_map/ppermute | solution.py:288
  16.1 4.2 %shard_map.74 = bf16[128,2048]{1,0:T(8,128)(2,1)} custom-call(bf16[1024,8192]{1,0:T(8,128)(2,1)} %refs_0_.7, f32[8,8,1024]{2,1,0:T(8,128)S(1)} %bitcast.37, bf16[128,1024]{1,0:T(8,128)(2,1)S(1)} %fusion.1.refs_2_), custom_call_target="tpu_custom_call" | custom-call | flops 536870912 | bytes 4194304 | tf_op jit(solution)/shard_map/pallas_call | solution.py:114
  20.3 1.5 %collective-permute-start.3 = (bf16[128,2048]{1,0:T(8,128)(2,1)}, bf16[128,2048]{1,0:T(8,128)(2,1)}, u32[]{:S(2)}, u32[]{:S(2)}) collective-permute-start(bf16[128,2048]{1,0:T(8,128)(2,1)} %shard_map.74), channel_id=1, source_target_pairs={{0,6},{1,7},{2,4},{3,5},{4,2},{5,3},{6,0},{7,1},{8,14},{9,15},{10,... | collective-permute-start | bytes 1572872 | tf_op jit(solution)/shard_map/ppermute | solution.py:288
  21.8 6.1 %shard_map.75 = (bf16[128,2048]{1,0:T(8,128)(2,1)}, bf16[128,2048]{1,0:T(8,128)(2,1)}) custom-call(bf16[1024,8192]{1,0:T(8,128)(2,1)} %refs_0_.7, f32[8,8,1024]{2,1,0:T(8,128)S(1)} %bitcast.38, bf16[128,1024]{1,0:T(8,128)(2,1)S(1)} %fusion.1.refs_2_), custom_call_target="tpu_custom_call" | custom-call | flops 1073741824 | bytes 8388608 | tf_op jit(solution)/shard_map/pallas_call | solution.py:114
  28.1 2.0 %collective-permute-start.10 = (bf16[128,2048]{1,0:T(8,128)(2,1)}, bf16[128,2048]{1,0:T(8,128)(2,1)}, u32[]{:S(2)}, u32[]{:S(2)}) collective-permute-start(bf16[128,2048]{1,0:T(8,128)(2,1)} %get-tuple-element.23), channel_id=1, source_target_pairs={{0,4},{1,5},{2,6},{3,7},{4,0},{5,1},{6,2},{7,3},{8,12},{9,13},{10,... | collective-permute-start | bytes 1572872 | tf_op jit(solution)/shard_map/ppermute | solution.py:288
  30.1 1.4 %add_convert_fusion.refs_4_ = bf16[256,1024]{1,0:T(8,128)(2,1)S(1)} fusion(f32[256,1024]{1,0:T(8,128)S(1)} %get-tuple-element.19, f32[256,1024]{1,0:T(8,128)} %collective-permute-done.6), kind=kLoop, calls=%fused_computation.2 | loop fusion | flops 524288 | bytes 2621440 | tf_op jit(solution)/shard_map/convert_element_type | solution.py:303
  31.4 2.8 %collective-permute-start.7 = (bf16[256,1024]{1,0:T(8,128)(2,1)S(1)}, bf16[256,1024]{1,0:T(8,128)(2,1)S(1)}, u32[]{:S(2)}, u32[]{:S(2)}) collective-permute-start(bf16[256,1024]{1,0:T(8,128)(2,1)S(1)} %add_convert_fusion.refs_4_), channel_id=1, source_target_pairs={{0,16},{1,17},{2,18},{3,19},{4,20},{5,21},{6,22},{7,23},{8,0},{9,1... | collective-permute-start | bytes 1572872 | tf_op jit(solution)/shard_map/ppermute | solution.py:288
  34.3 1.6 %collective-permute-start.1 = (s32[1,128]{1,0:T(1,128)S(1)}, s32[1,128]{1,0:T(1,128)S(1)}, u32[]{:S(2)}, u32[]{:S(2)}) collective-permute-start(s32[1,128]{1,0:T(1,128)S(1)} %bitcast.47), channel_id=1, source_target_pairs={{0,2},{1,3},{2,0},{3,1},{4,6},{5,7},{6,4},{7,5},{8,10},{9,11},{10,... | collective-permute-start | bytes 1544 | tf_op jit(solution)/shard_map/ppermute | solution.py:288
  35.8 9.9 %collective-permute-done.1 = s32[1,128]{1,0:T(1,128)S(1)} collective-permute-done((s32[1,128]{1,0:T(1,128)S(1)}, s32[1,128]{1,0:T(1,128)S(1)}, u32[]{:S(2)}, u32[]{:S(2)}) %collective-permute-start.1) | collective-permute-done | bytes 544 | tf_op jit(solution)/shard_map/ppermute | solution.py:288
  45.7 2.6 %collective-permute-start = (s32[1,128]{1,0:T(1,128)S(1)}, s32[1,128]{1,0:T(1,128)S(1)}, u32[]{:S(2)}, u32[]{:S(2)}) collective-permute-start(s32[1,128]{1,0:T(1,128)S(1)} %bitcast.48), channel_id=1, source_target_pairs={{0,6},{1,7},{2,4},{3,5},{4,2},{5,3},{6,0},{7,1},{8,14},{9,15},{10,... | collective-permute-start | bytes 1544 | tf_op jit(solution)/shard_map/ppermute | solution.py:288
  48.4 3.4 %shard_map.73.refs_0_ = bf16[128,2048]{1,0:T(8,128)(2,1)S(1)} custom-call(bf16[1024,8192]{1,0:T(8,128)(2,1)} %refs_0_.7, f32[8,8,1024]{2,1,0:T(8,128)S(1)} %bitcast.39, bf16[128,1024]{1,0:T(8,128)(2,1)S(1)} %fusion.1.refs_2_), custom_call_target="tpu_custom_call" | custom-call | flops 536870912 | bytes 4194304 | tf_op jit(solution)/shard_map/pallas_call | solution.py:114
  53.3 1.3 %collective-permute-start.8 = (bf16[256,1024]{1,0:T(8,128)(2,1)S(1)}, bf16[256,1024]{1,0:T(8,128)(2,1)S(1)}, u32[]{:S(2)}, u32[]{:S(2)}) collective-permute-start(bf16[256,1024]{1,0:T(8,128)(2,1)S(1)} %add_convert_fusion.refs_4_), channel_id=1, source_target_pairs={{8,24},{9,25},{10,26},{11,27},{12,28},{13,29},{14,30},{15,31},{16,... | collective-permute-start | bytes 1572872 | tf_op jit(solution)/shard_map/ppermute | solution.py:288
  55.3 6.1 %collective-permute-start.13 = (bf16[256,1024]{1,0:T(8,128)(2,1)S(1)}, bf16[256,1024]{1,0:T(8,128)(2,1)S(1)}, u32[]{:S(2)}, u32[]{:S(2)}) collective-permute-start(bf16[256,1024]{1,0:T(8,128)(2,1)S(1)} %broadcast_select_fusion), channel_id=1, source_target_pairs={{0,8},{1,9},{2,10},{3,11},{4,12},{5,13},{6,14},{7,15},{8,0},{9,1},... | collective-permute-start | bytes 1572872 | tf_op jit(solution)/shard_map/ppermute | solution.py:288
  62.1 8.7 %collective-permute-done.8.refs_6_ = bf16[256,1024]{1,0:T(8,128)(2,1)S(1)} collective-permute-done((bf16[256,1024]{1,0:T(8,128)(2,1)S(1)}, bf16[256,1024]{1,0:T(8,128)(2,1)S(1)}, u32[]{:S(2)}, u32[]{:S(2)}) %collective-permute-start.8) | collective-permute-done | bytes 524320 | tf_op jit(solution)/shard_map/ppermute | solution.py:288
  70.9 2.5 %near.2 = (f32[256,256]{1,0:T(8,128)S(1)}, bf16[256,1024]{1,0:T(8,128)(2,1)S(1)}, bf16[256,1024]{1,0:T(8,128)(2,1)S(1)}) custom-call(bf16[128,2048]{1,0:T(8,128)(2,1)S(1)} %shard_map.73.refs_0_, bf16[128,2048]{1,0:T(8,128)(2,1)} %collective-permute-done.3.refs_1_, bf16[128,2048]{1,0:T(8,128)(2,1)S(1)} %collective-permute-done.4.refs_2_, ...), custom_call_target="tpu_custom_call" | custom-call | flops 402653184 | bytes 1572864 | tf_op jit(solution)/shard_map/near/pallas_call | solution.py:189
  73.4 2.6 %near.3 = (f32[256,256]{1,0:T(8,128)S(1)}, bf16[256,1024]{1,0:T(8,128)(2,1)S(1)}, bf16[256,1024]{1,0:T(8,128)(2,1)S(1)}) custom-call(bf16[128,2048]{1,0:T(8,128)(2,1)} %collective-permute-done.9.refs_0_, bf16[128,2048]{1,0:T(8,128)(2,1)} %collective-permute-done.10.refs_1_, bf16[128,2048]{1,0:T(8,128)(2,1)S(1)} %collective-permute-done.11.refs_2_, ...), custom_call_target="tpu_custom_call" | custom-call | flops 402653184 | bytes 1572864 | tf_op jit(solution)/shard_map/near/pallas_call | solution.py:189
  76.0 5.1 %collective-permute-done.13.refs_7_ = bf16[256,1024]{1,0:T(8,128)(2,1)S(1)} collective-permute-done((bf16[256,1024]{1,0:T(8,128)(2,1)S(1)}, bf16[256,1024]{1,0:T(8,128)(2,1)S(1)}, u32[]{:S(2)}, u32[]{:S(2)}) %collective-permute-start.13) | collective-permute-done | bytes 524320 | tf_op jit(solution)/shard_map/ppermute | solution.py:288
  84.4 1.5 %collective-permute-start.15 = (bf16[256,256]{1,0:T(8,128)(2,1)S(1)}, bf16[256,256]{1,0:T(8,128)(2,1)S(1)}, u32[]{:S(2)}, u32[]{:S(2)}) collective-permute-start(bf16[256,256]{1,0:T(8,128)(2,1)S(1)} %get-tuple-element.30), channel_id=1, source_target_pairs={{0,2},{1,3},{2,0},{3,1},{4,6},{5,7},{6,4},{7,5},{8,10},{9,11},{10,... | collective-permute-start | bytes 393224 | tf_op jit(solution)/shard_map/ppermute | solution.py:288
  85.9 3.7 %collective-permute-done.17 = bf16[256,256]{1,0:T(8,128)(2,1)S(1)} collective-permute-done((bf16[256,256]{1,0:T(8,128)(2,1)S(1)}, bf16[256,256]{1,0:T(8,128)(2,1)S(1)}, u32[]{:S(2)}, u32[]{:S(2)}) %collective-permute-start.17) | collective-permute-done | bytes 131104 | tf_op jit(solution)/shard_map/ppermute | solution.py:288
  89.7 1.6 %collective-permute-done.16 = bf16[256,256]{1,0:T(8,128)(2,1)S(1)} collective-permute-done((bf16[256,256]{1,0:T(8,128)(2,1)S(1)}, bf16[256,256]{1,0:T(8,128)(2,1)S(1)}, u32[]{:S(2)}, u32[]{:S(2)}) %collective-permute-start.16) | collective-permute-done | bytes 131104 | tf_op jit(solution)/shard_map/ppermute | solution.py:288
  91.5 3.7 %collective-permute-start.20 = (bf16[64,384]{1,0:T(8,128)(2,1)S(1)}, bf16[64,384]{1,0:T(8,128)(2,1)S(1)}, u32[]{:S(2)}, u32[]{:S(2)}) collective-permute-start(bf16[64,384]{1,0:T(8,128)(2,1)S(1)} %bitcast.44), channel_id=1, source_target_pairs={{0,24},{1,25},{2,26},{3,27},{4,28},{5,29},{6,30},{7,31},{8,16},{9,... | collective-permute-start | bytes 147464 | tf_op jit(solution)/shard_map/ppermute | solution.py:288
  96.0 2.1 %collective-permute-done.20 = bf16[64,384]{1,0:T(8,128)(2,1)S(1)} collective-permute-done((bf16[64,384]{1,0:T(8,128)(2,1)S(1)}, bf16[64,384]{1,0:T(8,128)(2,1)S(1)}, u32[]{:S(2)}, u32[]{:S(2)}) %collective-permute-start.20) | collective-permute-done | bytes 49184 | tf_op jit(solution)/shard_map/ppermute | solution.py:288
  98.0 2.1 %collective-permute-done.19 = bf16[64,384]{1,0:T(8,128)(2,1)S(1)} collective-permute-done((bf16[64,384]{1,0:T(8,128)(2,1)S(1)}, bf16[64,384]{1,0:T(8,128)(2,1)S(1)}, u32[]{:S(2)}, u32[]{:S(2)}) %collective-permute-start.19) | collective-permute-done | bytes 49184 | tf_op jit(solution)/shard_map/ppermute | solution.py:288
  (50 shorter events, 8.8 us)
Async XLA Ops:
  0.0 16.0 %copy-start.1 = (s32[1,1024]{1,0:T(1,128)S(1)}, s32[1,1024]{1,0:T(1,128)}, u32[]{:S(2)}) copy-start(s32[1,1024]{1,0:T(1,128)} %param.9) | copy-start | bytes 12292
  0.0 16.1 %copy-start = (f32[64,1024]{1,0:T(8,128)S(1)}, f32[64,1024]{1,0:T(8,128)}, u32[]{:S(2)}) copy-start(f32[64,1024]{1,0:T(8,128)} %param.8) | copy-start | bytes 786436
  12.8 17.2 %collective-permute-start.6 = (f32[256,1024]{1,0:T(8,128)}, f32[256,1024]{1,0:T(8,128)}, u32[]{:S(2)}, u32[]{:S(2)}) collective-permute-start(f32[256,1024]{1,0:T(8,128)} %get-tuple-element.20), channel_id=1, source_target_pairs={{0,1},{1,0},{2,3},{3,2},{4,5},{5,4},{6,7},{7,6},{8,9},{9,8},{10,11... | collective-permute-start | bytes 3145736 | tf_op jit(solution)/shard_map/ppermute | solution.py:288
  13.4 20.8 %collective-permute-start.2 = (s32[1,128]{1,0:T(1,128)S(1)}, s32[1,128]{1,0:T(1,128)S(1)}, u32[]{:S(2)}, u32[]{:S(2)}) collective-permute-start(s32[1,128]{1,0:T(1,128)S(1)} %bitcast.46), channel_id=1, source_target_pairs={{0,4},{1,5},{2,6},{3,7},{4,0},{5,1},{6,2},{7,3},{8,12},{9,13},{10,... | collective-permute-start | bytes 1544 | tf_op jit(solution)/shard_map/ppermute | solution.py:288
  20.3 13.9 %copy-start.3 = (s32[4]{0:T(128)S(1)}, s32[4]{0:T(128)}, u32[]{:S(2)}) copy-start(s32[4]{0:T(128)} %constant.94.clone) | copy-start | bytes 52
  20.3 31.6 %collective-permute-start.3 = (bf16[128,2048]{1,0:T(8,128)(2,1)}, bf16[128,2048]{1,0:T(8,128)(2,1)}, u32[]{:S(2)}, u32[]{:S(2)}) collective-permute-start(bf16[128,2048]{1,0:T(8,128)(2,1)} %shard_map.74), channel_id=1, source_target_pairs={{0,6},{1,7},{2,4},{3,5},{4,2},{5,3},{6,0},{7,1},{8,14},{9,15},{10,... | collective-permute-start | bytes 1572872 | tf_op jit(solution)/shard_map/ppermute | solution.py:288
  27.9 24.7 %collective-permute-start.9 = (bf16[128,2048]{1,0:T(8,128)(2,1)}, bf16[128,2048]{1,0:T(8,128)(2,1)}, u32[]{:S(2)}, u32[]{:S(2)}) collective-permute-start(bf16[128,2048]{1,0:T(8,128)(2,1)} %get-tuple-element.22), channel_id=1, source_target_pairs={{0,2},{1,3},{2,0},{3,1},{4,6},{5,7},{6,4},{7,5},{8,10},{9,11},{10,... | collective-permute-start | bytes 1572872 | tf_op jit(solution)/shard_map/ppermute | solution.py:288
  28.1 24.7 %collective-permute-start.10 = (bf16[128,2048]{1,0:T(8,128)(2,1)}, bf16[128,2048]{1,0:T(8,128)(2,1)}, u32[]{:S(2)}, u32[]{:S(2)}) collective-permute-start(bf16[128,2048]{1,0:T(8,128)(2,1)} %get-tuple-element.23), channel_id=1, source_target_pairs={{0,4},{1,5},{2,6},{3,7},{4,0},{5,1},{6,2},{7,3},{8,12},{9,13},{10,... | collective-permute-start | bytes 1572872 | tf_op jit(solution)/shard_map/ppermute | solution.py:288
  31.4 21.8 %collective-permute-start.7 = (bf16[256,1024]{1,0:T(8,128)(2,1)S(1)}, bf16[256,1024]{1,0:T(8,128)(2,1)S(1)}, u32[]{:S(2)}, u32[]{:S(2)}) collective-permute-start(bf16[256,1024]{1,0:T(8,128)(2,1)S(1)} %add_convert_fusion.refs_4_), channel_id=1, source_target_pairs={{0,16},{1,17},{2,18},{3,19},{4,20},{5,21},{6,22},{7,23},{8,0},{9,1... | collective-permute-start | bytes 1572872 | tf_op jit(solution)/shard_map/ppermute | solution.py:288
  34.3 11.5 %collective-permute-start.1 = (s32[1,128]{1,0:T(1,128)S(1)}, s32[1,128]{1,0:T(1,128)S(1)}, u32[]{:S(2)}, u32[]{:S(2)}) collective-permute-start(s32[1,128]{1,0:T(1,128)S(1)} %bitcast.47), channel_id=1, source_target_pairs={{0,2},{1,3},{2,0},{3,1},{4,6},{5,7},{6,4},{7,5},{8,10},{9,11},{10,... | collective-permute-start | bytes 1544 | tf_op jit(solution)/shard_map/ppermute | solution.py:288
  45.7 6.1 %collective-permute-start = (s32[1,128]{1,0:T(1,128)S(1)}, s32[1,128]{1,0:T(1,128)S(1)}, u32[]{:S(2)}, u32[]{:S(2)}) collective-permute-start(s32[1,128]{1,0:T(1,128)S(1)} %bitcast.48), channel_id=1, source_target_pairs={{0,6},{1,7},{2,4},{3,5},{4,2},{5,3},{6,0},{7,1},{8,14},{9,15},{10,... | collective-permute-start | bytes 1544 | tf_op jit(solution)/shard_map/ppermute | solution.py:288
  51.8 2.8 %collective-permute-start.4 = (bf16[128,2048]{1,0:T(8,128)(2,1)S(1)}, bf16[128,2048]{1,0:T(8,128)(2,1)S(1)}, u32[]{:S(2)}, u32[]{:S(2)}) collective-permute-start(bf16[128,2048]{1,0:T(8,128)(2,1)S(1)} %shard_map.73.refs_0_), channel_id=1, source_target_pairs={{0,1},{1,0},{2,3},{3,2},{4,5},{5,4},{6,7},{7,6},{8,9},{9,8},{10,11... | collective-permute-start | bytes 1572872 | tf_op jit(solution)/shard_map/ppermute | solution.py:288
  51.9 3.4 %collective-permute-start.5 = (bf16[128,2048]{1,0:T(8,128)(2,1)}, bf16[128,2048]{1,0:T(8,128)(2,1)S(1)}, u32[]{:S(2)}, u32[]{:S(2)}) collective-permute-start(bf16[128,2048]{1,0:T(8,128)(2,1)} %collective-permute-done.3.refs_1_), channel_id=1, source_target_pairs={{0,1},{1,0},{2,3},{3,2},{4,5},{5,4},{6,7},{7,6},{8,9},{9,8},{10,11... | collective-permute-start | bytes 1572872 | tf_op jit(solution)/shard_map/ppermute | solution.py:288
  52.7 20.7 %collective-permute-start.11 = (bf16[128,2048]{1,0:T(8,128)(2,1)}, bf16[128,2048]{1,0:T(8,128)(2,1)S(1)}, u32[]{:S(2)}, u32[]{:S(2)}) collective-permute-start(bf16[128,2048]{1,0:T(8,128)(2,1)} %collective-permute-done.9.refs_0_), channel_id=1, source_target_pairs={{0,1},{1,0},{2,3},{3,2},{4,5},{5,4},{6,7},{7,6},{8,9},{9,8},{10,11... | collective-permute-start | bytes 1572872 | tf_op jit(solution)/shard_map/ppermute | solution.py:288
  52.8 20.6 %collective-permute-start.12 = (bf16[128,2048]{1,0:T(8,128)(2,1)}, bf16[128,2048]{1,0:T(8,128)(2,1)S(1)}, u32[]{:S(2)}, u32[]{:S(2)}) collective-permute-start(bf16[128,2048]{1,0:T(8,128)(2,1)} %collective-permute-done.10.refs_1_), channel_id=1, source_target_pairs={{0,1},{1,0},{2,3},{3,2},{4,5},{5,4},{6,7},{7,6},{8,9},{9,8},{10,11... | collective-permute-start | bytes 1572872 | tf_op jit(solution)/shard_map/ppermute | solution.py:288
  53.3 17.6 %collective-permute-start.8 = (bf16[256,1024]{1,0:T(8,128)(2,1)S(1)}, bf16[256,1024]{1,0:T(8,128)(2,1)S(1)}, u32[]{:S(2)}, u32[]{:S(2)}) collective-permute-start(bf16[256,1024]{1,0:T(8,128)(2,1)S(1)} %add_convert_fusion.refs_4_), channel_id=1, source_target_pairs={{8,24},{9,25},{10,26},{11,27},{12,28},{13,29},{14,30},{15,31},{16,... | collective-permute-start | bytes 1572872 | tf_op jit(solution)/shard_map/ppermute | solution.py:288
  54.6 21.4 %collective-permute-start.14 = (bf16[256,1024]{1,0:T(8,128)(2,1)S(1)}, bf16[256,1024]{1,0:T(8,128)(2,1)S(1)}, u32[]{:S(2)}, u32[]{:S(2)}) collective-permute-start(bf16[256,1024]{1,0:T(8,128)(2,1)S(1)} %add_convert_fusion.refs_4_), channel_id=1, source_target_pairs={{8,16},{9,17},{10,18},{11,19},{12,20},{13,21},{14,22},{15,23},{16,... | collective-permute-start | bytes 1572872 | tf_op jit(solution)/shard_map/ppermute | solution.py:288
  55.3 25.9 %collective-permute-start.13 = (bf16[256,1024]{1,0:T(8,128)(2,1)S(1)}, bf16[256,1024]{1,0:T(8,128)(2,1)S(1)}, u32[]{:S(2)}, u32[]{:S(2)}) collective-permute-start(bf16[256,1024]{1,0:T(8,128)(2,1)S(1)} %broadcast_select_fusion), channel_id=1, source_target_pairs={{0,8},{1,9},{2,10},{3,11},{4,12},{5,13},{6,14},{7,15},{8,0},{9,1},... | collective-permute-start | bytes 1572872 | tf_op jit(solution)/shard_map/ppermute | solution.py:288
  82.3 7.4 %collective-permute-start.17 = (bf16[256,256]{1,0:T(8,128)(2,1)S(1)}, bf16[256,256]{1,0:T(8,128)(2,1)S(1)}, u32[]{:S(2)}, u32[]{:S(2)}) collective-permute-start(bf16[256,256]{1,0:T(8,128)(2,1)S(1)} %get-tuple-element.32), channel_id=1, source_target_pairs={{0,6},{1,7},{2,4},{3,5},{4,2},{5,3},{6,0},{7,1},{8,14},{9,15},{10,... | collective-permute-start | bytes 393224 | tf_op jit(solution)/shard_map/ppermute | solution.py:288
  83.3 8.0 %collective-permute-start.16 = (bf16[256,256]{1,0:T(8,128)(2,1)S(1)}, bf16[256,256]{1,0:T(8,128)(2,1)S(1)}, u32[]{:S(2)}, u32[]{:S(2)}) collective-permute-start(bf16[256,256]{1,0:T(8,128)(2,1)S(1)} %get-tuple-element.31), channel_id=1, source_target_pairs={{0,4},{1,5},{2,6},{3,7},{4,0},{5,1},{6,2},{7,3},{8,12},{9,13},{10,... | collective-permute-start | bytes 393224 | tf_op jit(solution)/shard_map/ppermute | solution.py:288
  84.4 6.9 %collective-permute-start.15 = (bf16[256,256]{1,0:T(8,128)(2,1)S(1)}, bf16[256,256]{1,0:T(8,128)(2,1)S(1)}, u32[]{:S(2)}, u32[]{:S(2)}) collective-permute-start(bf16[256,256]{1,0:T(8,128)(2,1)S(1)} %get-tuple-element.30), channel_id=1, source_target_pairs={{0,2},{1,3},{2,0},{3,1},{4,6},{5,7},{6,4},{7,5},{8,10},{9,11},{10,... | collective-permute-start | bytes 393224 | tf_op jit(solution)/shard_map/ppermute | solution.py:288
  91.5 6.5 %collective-permute-start.20 = (bf16[64,384]{1,0:T(8,128)(2,1)S(1)}, bf16[64,384]{1,0:T(8,128)(2,1)S(1)}, u32[]{:S(2)}, u32[]{:S(2)}) collective-permute-start(bf16[64,384]{1,0:T(8,128)(2,1)S(1)} %bitcast.44), channel_id=1, source_target_pairs={{0,24},{1,25},{2,26},{3,27},{4,28},{5,29},{6,30},{7,31},{8,16},{9,... | collective-permute-start | bytes 147464 | tf_op jit(solution)/shard_map/ppermute | solution.py:288
  95.2 5.0 %collective-permute-start.19 = (bf16[64,384]{1,0:T(8,128)(2,1)S(1)}, bf16[64,384]{1,0:T(8,128)(2,1)S(1)}, u32[]{:S(2)}, u32[]{:S(2)}) collective-permute-start(bf16[64,384]{1,0:T(8,128)(2,1)S(1)} %bitcast.43), channel_id=1, source_target_pairs={{0,16},{1,17},{2,18},{3,19},{4,20},{5,21},{6,22},{7,23},{8,24},{9,... | collective-permute-start | bytes 147464 | tf_op jit(solution)/shard_map/ppermute | solution.py:288
  95.2 5.0 %collective-permute-start.18 = (bf16[64,384]{1,0:T(8,128)(2,1)S(1)}, bf16[64,384]{1,0:T(8,128)(2,1)S(1)}, u32[]{:S(2)}, u32[]{:S(2)}) collective-permute-start(bf16[64,384]{1,0:T(8,128)(2,1)S(1)} %bitcast.42), channel_id=1, source_target_pairs={{0,8},{1,9},{2,10},{3,11},{4,12},{5,13},{6,14},{7,15},{8,0},{9,1},... | collective-permute-start | bytes 147464 | tf_op jit(solution)/shard_map/ppermute | solution.py:288
  (1 other events, 13.4 us)

commit v3 on v2

--- a/solution.py
+++ b/solution.py
@@ -8,7 +8,7 @@
 QBLOCK = 128
 GRP_DEV = 128
 AXES = ("dp", "mp")
-LANES = 128
+META = 8
 
 
 ANYWHERE = pl.BlockSpec(memory_space=pl.ANY)
@@ -221,13 +221,13 @@
     for part, total in enumerate(totals):
         span = slice(start, start + total.shape[0])
         start += total.shape[0]
+        acc[span, :] = total[...]
         for i, (pair, block) in enumerate(zip(late, blocks)):
             _, here = hop_of(pair)
 
             @when(here)
             def _():
-                before = total[...] if i == 0 else acc[span, :]
-                acc[span, :] = before + contract(fars[part * len(late) + i][...], block[...])
+                acc[span, :] += contract(fars[part * len(late) + i][...], block[...])
 
     sending = jnp.dot(
         routing[...], acc[...].astype(jnp.bfloat16), preferred_element_type=jnp.float32
@@ -302,15 +302,12 @@
         block = block + to_lane(theirs[hop - 1], hop)
     block = block.astype(jnp.bfloat16)
     if line == 4:
-        inside = (at_line == 1) | (at_line == 2)
-        outward = {0: 2, 3: 1, 2: 3, 1: 0}
-        early = move(block, lambda s, t, m: (outward[s], t, m))
-        skip = move(block, lambda s, t, m: (s ^ 2, t, m) if s in (1, 2) else None)
+        early = move(block, lambda s, t, m: ((2, 0, 3, 1)[s], t, m))
+        skip = move(block, lambda s, t, m: ((1, 3, 0, 2)[s], t, m))
+        relay = move(early, lambda s, t, m: (s ^ 1, t, m) if s in (1, 2) else None)
         middle = move(block, lambda s, t, m: (s ^ 3, t, m) if s in (1, 2) else None)
-        onward = jnp.where(inside, early, block)
-        relay = move(onward, lambda s, t, m: (s ^ 1, t, m))
-        nearer = {(0, 0): block, (1, 2): early, (2, None): skip}
-        later = {(3, 1): relay, (None, 3): middle}
+        nearer = {(0, 0): block, (1, 2): early, (2, 1): skip}
+        later = {(3, None): relay, (None, 3): middle}
     else:
         nearer = {(0, 0): block}
         for hop in range(1, line):
@@ -345,11 +342,10 @@
     rows = jnp.arange(chips * per_chip, dtype=jnp.int32)[:, None]
     routing = (rows == row.reshape(1, -1)).astype(jnp.bfloat16)
     kept = rows[:per_chip] == row.reshape(1, -1)
-    meta = GRP_DEV + jnp.sum(
-        jnp.where(kept, inside_owner.reshape(1, -1) - GRP_DEV, 0), axis=1, keepdims=True
-    )
-    meta = jnp.broadcast_to(meta, (per_chip, LANES)).astype(jnp.bfloat16)
-    meta = meta.reshape(chips, line, capacity, LANES)
+    meta = GRP_DEV + jnp.sum(jnp.where(kept, inside_owner.reshape(1, -1) - GRP_DEV, 0), axis=1)
+    meta = meta.astype(jnp.bfloat16).reshape(chips, line, capacity)
+    meta = meta.transpose(1, 0, 2).reshape(line, 1, chips * capacity)
+    meta = jnp.pad(meta, ((0, 0), (0, META - 1), (0, share - chips * capacity)))
 
     late = tuple(later)
     totals, fars = [], []
@@ -371,19 +367,19 @@
     for hop in range(1, chips):
         whole = whole + to_plane(sending[hop], hop).astype(jnp.float32)
     whole = whole.astype(jnp.bfloat16).reshape(chips, line, capacity, share)
-    whole = jnp.concatenate([whole, meta], axis=3)
-    final = []
+    final, targets = [], []
     for hop in range(line):
-        own = lax.dynamic_index_in_dim(whole, jnp.bitwise_xor(at_line, hop), 1, keepdims=False)
-        own = own.reshape(chips * capacity, share + LANES)
-        final.append(to_line(own, hop) if hop else own)
+        owner = jnp.bitwise_xor(at_line, hop)
+        own = lax.dynamic_index_in_dim(whole, owner, 1, keepdims=False)
+        target = lax.dynamic_index_in_dim(meta, owner, 0, keepdims=False)
+        own = jnp.concatenate([own.reshape(chips * capacity, share), target], axis=0)
+        got = to_line(own, hop) if hop else own
+        final.append(got[: chips * capacity])
+        targets.append(got[chips * capacity : chips * capacity + 1, : chips * capacity])
     final = jnp.concatenate(final, axis=0)
-    chosen = (final[:, share:] == jnp.arange(LANES, dtype=jnp.bfloat16)[None, :]).astype(
-        jnp.bfloat16
-    )
-    return lax.dot_general(
-        chosen, final[:, :share], (((0,), (0,)), ((), ())), preferred_element_type=jnp.float32
-    )
+    targets = jnp.concatenate(targets, axis=1)
+    chosen = (jnp.arange(GRP_DEV, dtype=jnp.bfloat16)[:, None] == targets).astype(jnp.bfloat16)
+    return jnp.dot(chosen, final, preferred_element_type=jnp.float32)
 
 
 def solution(mesh):

time: 101 us -> 108 us (1.069)
  waiting for transfers between devices: 33.3 us -> 49 us
  starting transfers between devices: 31 us -> 22.6 us
    ppermute x21, waiting for transfers between devices: 33.3 us -> 49 us  [move(): return lax.ppermute(value, AXES, pairs)]
    ppermute x21, starting transfers between devices: 31 us -> 22.6 us  [move(): return lax.ppermute(value, AXES, pairs)]
  transfers between devices with their start and end apart: 21 -> 21, of which waited for: 7 -> 11; matrix products, arithmetic and copies ran while one was open for 3% -> 2% of each run, Pallas kernels for 19% -> 17%
where the time goes in v3:
time: 108 us
  waiting for transfers between devices  49 us (45%)
  Pallas kernels  32.1 us (30%)
  starting transfers between devices  22.6 us (21%)
  other arithmetic  2.56 us (2%)
    ppermute x21, waiting for transfers between devices, move(): return lax.ppermute(value, AXES, pairs)  49 us
    ppermute x21, starting transfers between devices, move(): return lax.ppermute(value, AXES, pairs)  22.6 us
    pallas_call x3, Pallas kernels, group_part(): pl.pallas_call(lambda *refs: group_kernel(*refs, peers=peers, chips=chips...  13 us
    pallas_call x1, Pallas kernels, precond_part(): pl.pallas_call(lambda *refs: precond_kernel(*refs, cut=cut, blocks=blocks...  12.8 us
    pallas_call x2, Pallas kernels, near_part(): pl.pallas_call(lambda *refs: near_kernel(*refs, hops=hops, late=late, chi...  5.14 us
  transfers between devices with their start and end apart: 21, of which 11 were waited for; matrix products, arithmetic and copies ran while one was open for 2% of the time, Pallas kernels for 17%

profile of v3, /device:TPU:0, one launch (start us, length us, event | category | flops | bytes accessed | tf_op | source)
XLA Modules:
  0.0 107.7 jit_solution(16712707972030747971)
XLA Ops:
  0.0 12.8 %precond.1 = (f32[256,1024]{1,0:T(8,128)S(1)}, f32[256,1024]{1,0:T(8,128)}) custom-call(bf16[512,8192]{1,0:T(8,128)(2,1)} %refs_0_.6, bf16[8192,1024]{1,0:T(8,128)(2,1)} %refs_1_.1), custom_call_target="tpu_custom_call" | custom-call | flops 8589934592 | bytes 25165824 | tf_op jit(solution)/shard_map/precond/pallas_call | solution.py:64
  13.5 5.3 %shard_map.75 = (bf16[128,2048]{1,0:T(8,128)(2,1)S(1)}, bf16[128,2048]{1,0:T(8,128)(2,1)S(1)}) custom-call(bf16[1024,8192]{1,0:T(8,128)(2,1)} %refs_0_.7, f32[8,8,1024]{2,1,0:T(8,128)S(1)} %bitcast.50, bf16[128,1024]{1,0:T(8,128)(2,1)S(1)} %fusion.1.refs_2_), custom_call_target="tpu_custom_call" | custom-call | flops 1073741824 | bytes 8388608 | tf_op jit(solution)/shard_map/pallas_call | solution.py:114
  18.8 2.5 %collective-permute-start.9 = (bf16[128,2048]{1,0:T(8,128)(2,1)S(1)}, bf16[128,2048]{1,0:T(8,128)(2,1)}, u32[]{:S(2)}, u32[]{:S(2)}) collective-permute-start(bf16[128,2048]{1,0:T(8,128)(2,1)S(1)} %get-tuple-element.22), channel_id=1, source_target_pairs={{0,2},{1,3},{2,0},{3,1},{4,6},{5,7},{6,4},{7,5},{8,10},{9,11},{10,... | collective-permute-start | bytes 1572872 | tf_op jit(solution)/shard_map/ppermute | solution.py:288
  21.3 1.5 %collective-permute-start.10 = (bf16[128,2048]{1,0:T(8,128)(2,1)S(1)}, bf16[128,2048]{1,0:T(8,128)(2,1)}, u32[]{:S(2)}, u32[]{:S(2)}) collective-permute-start(bf16[128,2048]{1,0:T(8,128)(2,1)S(1)} %get-tuple-element.23), channel_id=1, source_target_pairs={{0,4},{1,5},{2,6},{3,7},{4,0},{5,1},{6,2},{7,3},{8,12},{9,13},{10,... | collective-permute-start | bytes 1572872 | tf_op jit(solution)/shard_map/ppermute | solution.py:288
  22.9 4.2 %shard_map.74 = bf16[128,2048]{1,0:T(8,128)(2,1)} custom-call(bf16[1024,8192]{1,0:T(8,128)(2,1)} %refs_0_.7, f32[8,8,1024]{2,1,0:T(8,128)S(1)} %bitcast.51, bf16[128,1024]{1,0:T(8,128)(2,1)S(1)} %fusion.1.refs_2_), custom_call_target="tpu_custom_call" | custom-call | flops 536870912 | bytes 4194304 | tf_op jit(solution)/shard_map/pallas_call | solution.py:114
  27.1 3.0 %collective-permute-start.3 = (bf16[128,2048]{1,0:T(8,128)(2,1)}, bf16[128,2048]{1,0:T(8,128)(2,1)}, u32[]{:S(2)}, u32[]{:S(2)}) collective-permute-start(bf16[128,2048]{1,0:T(8,128)(2,1)} %shard_map.74), channel_id=1, source_target_pairs={{0,6},{1,7},{2,4},{3,5},{4,2},{5,3},{6,0},{7,1},{8,14},{9,15},{10,... | collective-permute-start | bytes 1572872 | tf_op jit(solution)/shard_map/ppermute | solution.py:288
  30.1 4.1 %collective-permute-done.9.refs_0_ = bf16[128,2048]{1,0:T(8,128)(2,1)} collective-permute-done((bf16[128,2048]{1,0:T(8,128)(2,1)S(1)}, bf16[128,2048]{1,0:T(8,128)(2,1)}, u32[]{:S(2)}, u32[]{:S(2)}) %collective-permute-start.9) | collective-permute-done | bytes 524320 | tf_op jit(solution)/shard_map/ppermute | solution.py:288
  34.2 12.5 %collective-permute-done.10.refs_1_ = bf16[128,2048]{1,0:T(8,128)(2,1)} collective-permute-done((bf16[128,2048]{1,0:T(8,128)(2,1)S(1)}, bf16[128,2048]{1,0:T(8,128)(2,1)}, u32[]{:S(2)}, u32[]{:S(2)}) %collective-permute-start.10) | collective-permute-done | bytes 524320 | tf_op jit(solution)/shard_map/ppermute | solution.py:288
  48.1 2.8 %collective-permute-start.7 = (bf16[256,1024]{1,0:T(8,128)(2,1)S(1)}, bf16[256,1024]{1,0:T(8,128)(2,1)S(1)}, u32[]{:S(2)}, u32[]{:S(2)}) collective-permute-start(bf16[256,1024]{1,0:T(8,128)(2,1)S(1)} %add_convert_fusion.refs_4_), channel_id=1, source_target_pairs={{0,16},{1,17},{2,18},{3,19},{4,20},{5,21},{6,22},{7,23},{8,0},{9,1... | collective-permute-start | bytes 1572872 | tf_op jit(solution)/shard_map/ppermute | solution.py:288
  50.9 3.5 %shard_map.73.refs_0_ = bf16[128,2048]{1,0:T(8,128)(2,1)S(1)} custom-call(bf16[1024,8192]{1,0:T(8,128)(2,1)} %refs_0_.7, f32[8,8,1024]{2,1,0:T(8,128)S(1)} %bitcast.52, bf16[128,1024]{1,0:T(8,128)(2,1)S(1)} %fusion.1.refs_2_), custom_call_target="tpu_custom_call" | custom-call | flops 536870912 | bytes 4194304 | tf_op jit(solution)/shard_map/pallas_call | solution.py:114
  54.5 3.5 %collective-permute-done.1 = s32[1,128]{1,0:T(1,128)S(1)} collective-permute-done((s32[1,128]{1,0:T(1,128)S(1)}, s32[1,128]{1,0:T(1,128)S(1)}, u32[]{:S(2)}, u32[]{:S(2)}) %collective-permute-start.1) | collective-permute-done | bytes 544 | tf_op jit(solution)/shard_map/ppermute | solution.py:288
  58.0 1.5 %collective-permute-start.2 = (s32[1,128]{1,0:T(1,128)S(1)}, s32[1,128]{1,0:T(1,128)S(1)}, u32[]{:S(2)}, u32[]{:S(2)}) collective-permute-start(s32[1,128]{1,0:T(1,128)S(1)} %bitcast.66), channel_id=1, source_target_pairs={{0,4},{1,5},{2,6},{3,7},{4,0},{5,1},{6,2},{7,3},{8,12},{9,13},{10,... | collective-permute-start | bytes 1544 | tf_op jit(solution)/shard_map/ppermute | solution.py:288
  59.6 2.0 %collective-permute-done.2 = s32[1,128]{1,0:T(1,128)S(1)} collective-permute-done((s32[1,128]{1,0:T(1,128)S(1)}, s32[1,128]{1,0:T(1,128)S(1)}, u32[]{:S(2)}, u32[]{:S(2)}) %collective-permute-start.2) | collective-permute-done | bytes 544 | tf_op jit(solution)/shard_map/ppermute | solution.py:288
  65.2 13.0 %collective-permute-done.8.refs_6_ = bf16[256,1024]{1,0:T(8,128)(2,1)S(1)} collective-permute-done((bf16[256,1024]{1,0:T(8,128)(2,1)S(1)}, bf16[256,1024]{1,0:T(8,128)(2,1)S(1)}, u32[]{:S(2)}, u32[]{:S(2)}) %collective-permute-start.8) | collective-permute-done | bytes 524320 | tf_op jit(solution)/shard_map/ppermute | solution.py:288
  78.2 2.8 %near.3 = (f32[256,256]{1,0:T(8,128)S(1)}, bf16[256,1024]{1,0:T(8,128)(2,1)S(1)}, bf16[256,1024]{1,0:T(8,128)(2,1)S(1)}) custom-call(bf16[128,2048]{1,0:T(8,128)(2,1)} %collective-permute-done.9.refs_0_, bf16[128,2048]{1,0:T(8,128)(2,1)} %collective-permute-done.10.refs_1_, bf16[128,2048]{1,0:T(8,128)(2,1)} %collective-permute-done.11.refs_2_, ...), custom_call_target="tpu_custom_call" | custom-call | flops 402653184 | bytes 1572864 | tf_op jit(solution)/shard_map/near/pallas_call | solution.py:189
  81.0 2.3 %near.2 = (f32[256,256]{1,0:T(8,128)S(1)}, bf16[256,1024]{1,0:T(8,128)(2,1)S(1)}, bf16[256,1024]{1,0:T(8,128)(2,1)S(1)}) custom-call(bf16[128,2048]{1,0:T(8,128)(2,1)S(1)} %shard_map.73.refs_0_, bf16[128,2048]{1,0:T(8,128)(2,1)} %collective-permute-done.3.refs_1_, bf16[128,2048]{1,0:T(8,128)(2,1)S(1)} %collective-permute-done.4.refs_2_, ...), custom_call_target="tpu_custom_call" | custom-call | flops 402653184 | bytes 1572864 | tf_op jit(solution)/shard_map/near/pallas_call | solution.py:189
  83.4 5.1 %collective-permute-done.13.refs_7_ = bf16[256,1024]{1,0:T(8,128)(2,1)S(1)} collective-permute-done((bf16[256,1024]{1,0:T(8,128)(2,1)S(1)}, bf16[256,1024]{1,0:T(8,128)(2,1)S(1)}, u32[]{:S(2)}, u32[]{:S(2)}) %collective-permute-start.13) | collective-permute-done | bytes 524320 | tf_op jit(solution)/shard_map/ppermute | solution.py:288
  89.7 2.0 %collective-permute-start.16 = (bf16[256,256]{1,0:T(8,128)(2,1)S(1)}, bf16[256,256]{1,0:T(8,128)(2,1)S(1)}, u32[]{:S(2)}, u32[]{:S(2)}) collective-permute-start(bf16[256,256]{1,0:T(8,128)(2,1)S(1)} %get-tuple-element.31), channel_id=1, source_target_pairs={{0,4},{1,5},{2,6},{3,7},{4,0},{5,1},{6,2},{7,3},{8,12},{9,13},{10,... | collective-permute-start | bytes 393224 | tf_op jit(solution)/shard_map/ppermute | solution.py:288
  91.8 1.4 %collective-permute-start.17 = (bf16[256,256]{1,0:T(8,128)(2,1)S(1)}, bf16[256,256]{1,0:T(8,128)(2,1)S(1)}, u32[]{:S(2)}, u32[]{:S(2)}) collective-permute-start(bf16[256,256]{1,0:T(8,128)(2,1)S(1)} %get-tuple-element.32), channel_id=1, source_target_pairs={{0,6},{1,7},{2,4},{3,5},{4,2},{5,3},{6,0},{7,1},{8,14},{9,15},{10,... | collective-permute-start | bytes 393224 | tf_op jit(solution)/shard_map/ppermute | solution.py:288
  93.4 2.6 %collective-permute-done.15 = bf16[256,256]{1,0:T(8,128)(2,1)S(1)} collective-permute-done((bf16[256,256]{1,0:T(8,128)(2,1)S(1)}, bf16[256,256]{1,0:T(8,128)(2,1)S(1)}, u32[]{:S(2)}, u32[]{:S(2)}) %collective-permute-start.15) | collective-permute-done | bytes 131104 | tf_op jit(solution)/shard_map/ppermute | solution.py:288
  97.3 1.6 %collective-permute-done.17 = bf16[256,256]{1,0:T(8,128)(2,1)S(1)} collective-permute-done((bf16[256,256]{1,0:T(8,128)(2,1)S(1)}, bf16[256,256]{1,0:T(8,128)(2,1)S(1)}, u32[]{:S(2)}, u32[]{:S(2)}) %collective-permute-start.17) | collective-permute-done | bytes 131104 | tf_op jit(solution)/shard_map/ppermute | solution.py:288
  99.1 1.9 %collective-permute-start.19 = (bf16[72,256]{1,0:T(8,128)(2,1)S(1)}, bf16[72,256]{1,0:T(8,128)(2,1)S(1)}, u32[]{:S(2)}, u32[]{:S(2)}) collective-permute-start(bf16[72,256]{1,0:T(8,128)(2,1)S(1)} %pad_maximum_fusion.1), channel_id=1, source_target_pairs={{0,16},{1,17},{2,18},{3,19},{4,20},{5,21},{6,22},{7,23},{8,24},{9,... | collective-permute-start | bytes 110600 | tf_op jit(solution)/shard_map/ppermute | solution.py:288
  101.0 2.5 %collective-permute-start.20 = (bf16[72,256]{1,0:T(8,128)(2,1)S(1)}, bf16[72,256]{1,0:T(8,128)(2,1)S(1)}, u32[]{:S(2)}, u32[]{:S(2)}) collective-permute-start(bf16[72,256]{1,0:T(8,128)(2,1)S(1)} %pad_maximum_fusion.2), channel_id=1, source_target_pairs={{0,24},{1,25},{2,26},{3,27},{4,28},{5,29},{6,30},{7,31},{8,16},{9,... | collective-permute-start | bytes 110600 | tf_op jit(solution)/shard_map/ppermute | solution.py:288
  104.0 2.7 %collective-permute-done.20 = bf16[72,256]{1,0:T(8,128)(2,1)S(1)} collective-permute-done((bf16[72,256]{1,0:T(8,128)(2,1)S(1)}, bf16[72,256]{1,0:T(8,128)(2,1)S(1)}, u32[]{:S(2)}, u32[]{:S(2)}) %collective-permute-start.20) | collective-permute-done | bytes 36896 | tf_op jit(solution)/shard_map/ppermute | solution.py:288
  (66 shorter events, 10.0 us)
Async XLA Ops:
  0.0 13.4 %copy-start.1 = (s32[1,1024]{1,0:T(1,128)S(1)}, s32[1,1024]{1,0:T(1,128)}, u32[]{:S(2)}) copy-start(s32[1,1024]{1,0:T(1,128)} %param.9) | copy-start | bytes 12292
  0.0 13.4 %copy-start = (f32[64,1024]{1,0:T(8,128)S(1)}, f32[64,1024]{1,0:T(8,128)}, u32[]{:S(2)}) copy-start(f32[64,1024]{1,0:T(8,128)} %param.8) | copy-start | bytes 786436
  12.8 33.9 %collective-permute-start.6 = (f32[256,1024]{1,0:T(8,128)}, f32[256,1024]{1,0:T(8,128)}, u32[]{:S(2)}, u32[]{:S(2)}) collective-permute-start(f32[256,1024]{1,0:T(8,128)} %get-tuple-element.20), channel_id=1, source_target_pairs={{0,1},{1,0},{2,3},{3,2},{4,5},{5,4},{6,7},{7,6},{8,9},{9,8},{10,11... | collective-permute-start | bytes 3145736 | tf_op jit(solution)/shard_map/ppermute | solution.py:288
  18.8 15.4 %collective-permute-start.9 = (bf16[128,2048]{1,0:T(8,128)(2,1)S(1)}, bf16[128,2048]{1,0:T(8,128)(2,1)}, u32[]{:S(2)}, u32[]{:S(2)}) collective-permute-start(bf16[128,2048]{1,0:T(8,128)(2,1)S(1)} %get-tuple-element.22), channel_id=1, source_target_pairs={{0,2},{1,3},{2,0},{3,1},{4,6},{5,7},{6,4},{7,5},{8,10},{9,11},{10,... | collective-permute-start | bytes 1572872 | tf_op jit(solution)/shard_map/ppermute | solution.py:288
  21.3 25.4 %collective-permute-start.10 = (bf16[128,2048]{1,0:T(8,128)(2,1)S(1)}, bf16[128,2048]{1,0:T(8,128)(2,1)}, u32[]{:S(2)}, u32[]{:S(2)}) collective-permute-start(bf16[128,2048]{1,0:T(8,128)(2,1)S(1)} %get-tuple-element.23), channel_id=1, source_target_pairs={{0,4},{1,5},{2,6},{3,7},{4,0},{5,1},{6,2},{7,3},{8,12},{9,13},{10,... | collective-permute-start | bytes 1572872 | tf_op jit(solution)/shard_map/ppermute | solution.py:288
  22.9 28.1 %copy-start.3 = (s32[4]{0:T(128)S(1)}, s32[4]{0:T(128)}, u32[]{:S(2)}) copy-start(s32[4]{0:T(128)} %constant.106.clone) | copy-start | bytes 52
  22.9 31.5 %collective-permute-start = (s32[1,128]{1,0:T(1,128)S(1)}, s32[1,128]{1,0:T(1,128)S(1)}, u32[]{:S(2)}, u32[]{:S(2)}) collective-permute-start(s32[1,128]{1,0:T(1,128)S(1)} %bitcast.64), channel_id=1, source_target_pairs={{0,6},{1,7},{2,4},{3,5},{4,2},{5,3},{6,0},{7,1},{8,14},{9,15},{10,... | collective-permute-start | bytes 1544 | tf_op jit(solution)/shard_map/ppermute | solution.py:288
  27.1 34.7 %collective-permute-start.3 = (bf16[128,2048]{1,0:T(8,128)(2,1)}, bf16[128,2048]{1,0:T(8,128)(2,1)}, u32[]{:S(2)}, u32[]{:S(2)}) collective-permute-start(bf16[128,2048]{1,0:T(8,128)(2,1)} %shard_map.74), channel_id=1, source_target_pairs={{0,6},{1,7},{2,4},{3,5},{4,2},{5,3},{6,0},{7,1},{8,14},{9,15},{10,... | collective-permute-start | bytes 1572872 | tf_op jit(solution)/shard_map/ppermute | solution.py:288
  34.2 28.2 %collective-permute-start.11 = (bf16[128,2048]{1,0:T(8,128)(2,1)}, bf16[128,2048]{1,0:T(8,128)(2,1)}, u32[]{:S(2)}, u32[]{:S(2)}) collective-permute-start(bf16[128,2048]{1,0:T(8,128)(2,1)} %collective-permute-done.9.refs_0_), channel_id=1, source_target_pairs={{0,1},{1,0},{2,3},{3,2},{4,5},{5,4},{6,7},{7,6},{8,9},{9,8},{10,11... | collective-permute-start | bytes 1572872 | tf_op jit(solution)/shard_map/ppermute | solution.py:288
  46.7 15.7 %collective-permute-start.12 = (bf16[128,2048]{1,0:T(8,128)(2,1)}, bf16[128,2048]{1,0:T(8,128)(2,1)}, u32[]{:S(2)}, u32[]{:S(2)}) collective-permute-start(bf16[128,2048]{1,0:T(8,128)(2,1)} %collective-permute-done.10.refs_1_), channel_id=1, source_target_pairs={{0,1},{1,0},{2,3},{3,2},{4,5},{5,4},{6,7},{7,6},{8,9},{9,8},{10,11... | collective-permute-start | bytes 1572872 | tf_op jit(solution)/shard_map/ppermute | solution.py:288
  48.1 15.1 %collective-permute-start.7 = (bf16[256,1024]{1,0:T(8,128)(2,1)S(1)}, bf16[256,1024]{1,0:T(8,128)(2,1)S(1)}, u32[]{:S(2)}, u32[]{:S(2)}) collective-permute-start(bf16[256,1024]{1,0:T(8,128)(2,1)S(1)} %add_convert_fusion.refs_4_), channel_id=1, source_target_pairs={{0,16},{1,17},{2,18},{3,19},{4,20},{5,21},{6,22},{7,23},{8,0},{9,1... | collective-permute-start | bytes 1572872 | tf_op jit(solution)/shard_map/ppermute | solution.py:288
  54.4 3.6 %collective-permute-start.1 = (s32[1,128]{1,0:T(1,128)S(1)}, s32[1,128]{1,0:T(1,128)S(1)}, u32[]{:S(2)}, u32[]{:S(2)}) collective-permute-start(s32[1,128]{1,0:T(1,128)S(1)} %bitcast.65), channel_id=1, source_target_pairs={{0,2},{1,3},{2,0},{3,1},{4,6},{5,7},{6,4},{7,5},{8,10},{9,11},{10,... | collective-permute-start | bytes 1544 | tf_op jit(solution)/shard_map/ppermute | solution.py:288
  58.0 3.6 %collective-permute-start.2 = (s32[1,128]{1,0:T(1,128)S(1)}, s32[1,128]{1,0:T(1,128)S(1)}, u32[]{:S(2)}, u32[]{:S(2)}) collective-permute-start(s32[1,128]{1,0:T(1,128)S(1)} %bitcast.66), channel_id=1, source_target_pairs={{0,4},{1,5},{2,6},{3,7},{4,0},{5,1},{6,2},{7,3},{8,12},{9,13},{10,... | collective-permute-start | bytes 1544 | tf_op jit(solution)/shard_map/ppermute | solution.py:288
  61.6 19.4 %collective-permute-start.4 = (bf16[128,2048]{1,0:T(8,128)(2,1)S(1)}, bf16[128,2048]{1,0:T(8,128)(2,1)S(1)}, u32[]{:S(2)}, u32[]{:S(2)}) collective-permute-start(bf16[128,2048]{1,0:T(8,128)(2,1)S(1)} %shard_map.73.refs_0_), channel_id=1, source_target_pairs={{0,1},{1,0},{2,3},{3,2},{4,5},{5,4},{6,7},{7,6},{8,9},{9,8},{10,11... | collective-permute-start | bytes 1572872 | tf_op jit(solution)/shard_map/ppermute | solution.py:288
  61.9 19.1 %collective-permute-start.5 = (bf16[128,2048]{1,0:T(8,128)(2,1)}, bf16[128,2048]{1,0:T(8,128)(2,1)S(1)}, u32[]{:S(2)}, u32[]{:S(2)}) collective-permute-start(bf16[128,2048]{1,0:T(8,128)(2,1)} %collective-permute-done.3.refs_1_), channel_id=1, source_target_pairs={{0,1},{1,0},{2,3},{3,2},{4,5},{5,4},{6,7},{7,6},{8,9},{9,8},{10,11... | collective-permute-start | bytes 1572872 | tf_op jit(solution)/shard_map/ppermute | solution.py:288
  62.5 15.7 %collective-permute-start.8 = (bf16[256,1024]{1,0:T(8,128)(2,1)S(1)}, bf16[256,1024]{1,0:T(8,128)(2,1)S(1)}, u32[]{:S(2)}, u32[]{:S(2)}) collective-permute-start(bf16[256,1024]{1,0:T(8,128)(2,1)S(1)} %add_convert_fusion.refs_4_), channel_id=1, source_target_pairs={{0,8},{1,9},{2,10},{3,11},{4,12},{5,13},{6,14},{7,15},{8,24},{9,25... | collective-permute-start | bytes 1572872 | tf_op jit(solution)/shard_map/ppermute | solution.py:288
  62.5 20.9 %collective-permute-start.14 = (bf16[256,1024]{1,0:T(8,128)(2,1)S(1)}, bf16[256,1024]{1,0:T(8,128)(2,1)S(1)}, u32[]{:S(2)}, u32[]{:S(2)}) collective-permute-start(bf16[256,1024]{1,0:T(8,128)(2,1)S(1)} %add_convert_fusion.refs_4_), channel_id=1, source_target_pairs={{8,16},{9,17},{10,18},{11,19},{12,20},{13,21},{14,22},{15,23},{16,... | collective-permute-start | bytes 1572872 | tf_op jit(solution)/shard_map/ppermute | solution.py:288
  63.2 25.3 %collective-permute-start.13 = (bf16[256,1024]{1,0:T(8,128)(2,1)S(1)}, bf16[256,1024]{1,0:T(8,128)(2,1)S(1)}, u32[]{:S(2)}, u32[]{:S(2)}) collective-permute-start(bf16[256,1024]{1,0:T(8,128)(2,1)S(1)} %collective-permute-done.7.refs_5_), channel_id=1, source_target_pairs={{8,0},{9,1},{10,2},{11,3},{12,4},{13,5},{14,6},{15,7},{16,24},{17,... | collective-permute-start | bytes 1572872 | tf_op jit(solution)/shard_map/ppermute | solution.py:288
  89.6 6.4 %collective-permute-start.15 = (bf16[256,256]{1,0:T(8,128)(2,1)S(1)}, bf16[256,256]{1,0:T(8,128)(2,1)S(1)}, u32[]{:S(2)}, u32[]{:S(2)}) collective-permute-start(bf16[256,256]{1,0:T(8,128)(2,1)S(1)} %get-tuple-element.30), channel_id=1, source_target_pairs={{0,2},{1,3},{2,0},{3,1},{4,6},{5,7},{6,4},{7,5},{8,10},{9,11},{10,... | collective-permute-start | bytes 393224 | tf_op jit(solution)/shard_map/ppermute | solution.py:288
  89.7 7.5 %collective-permute-start.16 = (bf16[256,256]{1,0:T(8,128)(2,1)S(1)}, bf16[256,256]{1,0:T(8,128)(2,1)S(1)}, u32[]{:S(2)}, u32[]{:S(2)}) collective-permute-start(bf16[256,256]{1,0:T(8,128)(2,1)S(1)} %get-tuple-element.31), channel_id=1, source_target_pairs={{0,4},{1,5},{2,6},{3,7},{4,0},{5,1},{6,2},{7,3},{8,12},{9,13},{10,... | collective-permute-start | bytes 393224 | tf_op jit(solution)/shard_map/ppermute | solution.py:288
  91.8 7.1 %collective-permute-start.17 = (bf16[256,256]{1,0:T(8,128)(2,1)S(1)}, bf16[256,256]{1,0:T(8,128)(2,1)S(1)}, u32[]{:S(2)}, u32[]{:S(2)}) collective-permute-start(bf16[256,256]{1,0:T(8,128)(2,1)S(1)} %get-tuple-element.32), channel_id=1, source_target_pairs={{0,6},{1,7},{2,4},{3,5},{4,2},{5,3},{6,0},{7,1},{8,14},{9,15},{10,... | collective-permute-start | bytes 393224 | tf_op jit(solution)/shard_map/ppermute | solution.py:288
  99.0 4.5 %collective-permute-start.18 = (bf16[72,256]{1,0:T(8,128)(2,1)S(1)}, bf16[72,256]{1,0:T(8,128)(2,1)S(1)}, u32[]{:S(2)}, u32[]{:S(2)}) collective-permute-start(bf16[72,256]{1,0:T(8,128)(2,1)S(1)} %pad_maximum_fusion), channel_id=1, source_target_pairs={{0,8},{1,9},{2,10},{3,11},{4,12},{5,13},{6,14},{7,15},{8,0},{9,1},... | collective-permute-start | bytes 110600 | tf_op jit(solution)/shard_map/ppermute | solution.py:288
  99.1 4.9 %collective-permute-start.19 = (bf16[72,256]{1,0:T(8,128)(2,1)S(1)}, bf16[72,256]{1,0:T(8,128)(2,1)S(1)}, u32[]{:S(2)}, u32[]{:S(2)}) collective-permute-start(bf16[72,256]{1,0:T(8,128)(2,1)S(1)} %pad_maximum_fusion.1), channel_id=1, source_target_pairs={{0,16},{1,17},{2,18},{3,19},{4,20},{5,21},{6,22},{7,23},{8,24},{9,... | collective-permute-start | bytes 110600 | tf_op jit(solution)/shard_map/ppermute | solution.py:288
  101.0 5.8 %collective-permute-start.20 = (bf16[72,256]{1,0:T(8,128)(2,1)S(1)}, bf16[72,256]{1,0:T(8,128)(2,1)S(1)}, u32[]{:S(2)}, u32[]{:S(2)}) collective-permute-start(bf16[72,256]{1,0:T(8,128)(2,1)S(1)} %pad_maximum_fusion.2), channel_id=1, source_target_pairs={{0,24},{1,25},{2,26},{3,27},{4,28},{5,29},{6,30},{7,31},{8,16},{9,... | collective-permute-start | bytes 110600 | tf_op jit(solution)/shard_map/ppermute | solution.py:288
  (1 other events, 9.4 us)

commit v4 on v3

--- a/solution.py
+++ b/solution.py
@@ -84,23 +84,25 @@
 def group_kernel(grads, scales, onehot, *refs, peers, chips, columns, width):
     outs, buffer, sems = refs[:-2], refs[-2], refs[-1]
     rows = buffer.shape[1]
-    blocks = width // QBLOCK
     copies = []
     for out, peer in zip(outs, peers):
         for c in range(columns):
             column = c * chips + jnp.bitwise_xor(lax.axis_index("dp") % chips, peer)
-            copy = pltpu.make_async_copy(
-                grads.at[:, pl.ds(pl.multiple_of(column * width, width), width)],
-                buffer.at[len(copies)],
-                sems.at[len(copies)],
-            )
-            copy.start()
-            copies.append((copy, out, column, c * width))
-    for i, (copy, out, column, at) in enumerate(copies):
+            cut = width if copies else width // 2
+            for first in range(0, width, cut):
+                at = len(copies)
+                slot = buffer.at[c + columns * peers.index(peer), :, pl.ds(first, cut)]
+                start = pl.multiple_of(column * width + first, cut)
+                copy = pltpu.make_async_copy(grads.at[:, pl.ds(start, cut)], slot, sems.at[at])
+                copy.start()
+                copies.append((copy, slot, out, column, first, cut, c * width + first))
+    for copy, slot, out, column, first, cut, at in copies:
         copy.wait()
-        turned = buffer[i].T.astype(jnp.float32).reshape(blocks, QBLOCK, rows)
-        dequant = (turned * scales[column][:, None, :]).astype(jnp.bfloat16).reshape(width, rows)
-        out[:, at : at + width] = lax.dot_general(
+        blocks = cut // QBLOCK
+        turned = slot[...].T.astype(jnp.float32).reshape(blocks, QBLOCK, rows)
+        steps = scales[column][first // QBLOCK : first // QBLOCK + blocks, :]
+        dequant = (turned * steps[:, None, :]).astype(jnp.bfloat16).reshape(cut, rows)
+        out[:, at : at + cut] = lax.dot_general(
             onehot[...], dequant, (((1,), (1,)), ((), ())), preferred_element_type=jnp.float32
         ).astype(jnp.bfloat16)
 
@@ -119,7 +121,7 @@
         out_specs=[ON_CHIP for _ in peers],
         scratch_shapes=[
             pltpu.VMEM((count, rows, width), grads.dtype),
-            pltpu.SemaphoreType.DMA((count,)),
+            pltpu.SemaphoreType.DMA((count + 1,)),
         ],
         out_shape=[pltpu.VMEM(shape, jnp.bfloat16) for _ in peers],
         cost_estimate=pl.CostEstimate(

time: 108 us -> 108 us (level)
  no operation moved by 1% of the time
where the time goes in v4:
time: 108 us; the launch traced here: 107 us
  waiting for transfers between devices  49.2 us (46%)
  Pallas kernels  31.7 us (29%)
  starting transfers between devices  22.6 us (21%)
  other arithmetic  2.56 us (2%)
    ppermute x21, waiting for transfers between devices, move(): return lax.ppermute(value, AXES, pairs)  49.2 us
    ppermute x21, starting transfers between devices, move(): return lax.ppermute(value, AXES, pairs)  22.6 us
    pallas_call x1, Pallas kernels, precond_part(): pl.pallas_call(lambda *refs: precond_kernel(*refs, cut=cut, blocks=blocks...  12.8 us
    pallas_call x3, Pallas kernels, group_part(): pl.pallas_call(lambda *refs: group_kernel(*refs, peers=peers, chips=chips...  12.6 us
    pallas_call x2, Pallas kernels, near_part(): pl.pallas_call(lambda *refs: near_kernel(*refs, hops=hops, late=late, chi...  5.14 us
  transfers between devices with their start and end apart: 21, of which 11 were waited for; matrix products, arithmetic and copies ran while one was open for 2% of the time, Pallas kernels for 17%

profile of v4, /device:TPU:0, one launch (start us, length us, event | category | flops | bytes accessed | tf_op | source)
XLA Modules:
  0.0 107.4 jit_solution(7080207060164078633)
XLA Ops:
  0.0 12.8 %precond.1 = (f32[256,1024]{1,0:T(8,128)S(1)}, f32[256,1024]{1,0:T(8,128)}) custom-call(bf16[512,8192]{1,0:T(8,128)(2,1)} %refs_0_.6, bf16[8192,1024]{1,0:T(8,128)(2,1)} %refs_1_.1), custom_call_target="tpu_custom_call" | custom-call | flops 8589934592 | bytes 25165824 | tf_op jit(solution)/shard_map/precond/pallas_call | solution.py:64
  13.5 5.2 %shard_map.75 = (bf16[128,2048]{1,0:T(8,128)(2,1)S(1)}, bf16[128,2048]{1,0:T(8,128)(2,1)S(1)}) custom-call(bf16[1024,8192]{1,0:T(8,128)(2,1)} %refs_0_.7, f32[8,8,1024]{2,1,0:T(8,128)S(1)} %bitcast.50, bf16[128,1024]{1,0:T(8,128)(2,1)S(1)} %fusion.1.refs_2_), custom_call_target="tpu_custom_call" | custom-call | flops 1073741824 | bytes 8388608 | tf_op jit(solution)/shard_map/pallas_call | solution.py:116
  18.6 2.5 %collective-permute-start.9 = (bf16[128,2048]{1,0:T(8,128)(2,1)S(1)}, bf16[128,2048]{1,0:T(8,128)(2,1)}, u32[]{:S(2)}, u32[]{:S(2)}) collective-permute-start(bf16[128,2048]{1,0:T(8,128)(2,1)S(1)} %get-tuple-element.22), channel_id=1, source_target_pairs={{0,2},{1,3},{2,0},{3,1},{4,6},{5,7},{6,4},{7,5},{8,10},{9,11},{10,... | collective-permute-start | bytes 1572872 | tf_op jit(solution)/shard_map/ppermute | solution.py:290
  21.2 1.5 %collective-permute-start.10 = (bf16[128,2048]{1,0:T(8,128)(2,1)S(1)}, bf16[128,2048]{1,0:T(8,128)(2,1)}, u32[]{:S(2)}, u32[]{:S(2)}) collective-permute-start(bf16[128,2048]{1,0:T(8,128)(2,1)S(1)} %get-tuple-element.23), channel_id=1, source_target_pairs={{0,4},{1,5},{2,6},{3,7},{4,0},{5,1},{6,2},{7,3},{8,12},{9,13},{10,... | collective-permute-start | bytes 1572872 | tf_op jit(solution)/shard_map/ppermute | solution.py:290
  22.8 4.1 %shard_map.74 = bf16[128,2048]{1,0:T(8,128)(2,1)} custom-call(bf16[1024,8192]{1,0:T(8,128)(2,1)} %refs_0_.7, f32[8,8,1024]{2,1,0:T(8,128)S(1)} %bitcast.51, bf16[128,1024]{1,0:T(8,128)(2,1)S(1)} %fusion.1.refs_2_), custom_call_target="tpu_custom_call" | custom-call | flops 536870912 | bytes 4194304 | tf_op jit(solution)/shard_map/pallas_call | solution.py:116
  26.9 3.0 %collective-permute-start.3 = (bf16[128,2048]{1,0:T(8,128)(2,1)}, bf16[128,2048]{1,0:T(8,128)(2,1)}, u32[]{:S(2)}, u32[]{:S(2)}) collective-permute-start(bf16[128,2048]{1,0:T(8,128)(2,1)} %shard_map.74), channel_id=1, source_target_pairs={{0,6},{1,7},{2,4},{3,5},{4,2},{5,3},{6,0},{7,1},{8,14},{9,15},{10,... | collective-permute-start | bytes 1572872 | tf_op jit(solution)/shard_map/ppermute | solution.py:290
  29.8 4.2 %collective-permute-done.9.refs_0_ = bf16[128,2048]{1,0:T(8,128)(2,1)} collective-permute-done((bf16[128,2048]{1,0:T(8,128)(2,1)S(1)}, bf16[128,2048]{1,0:T(8,128)(2,1)}, u32[]{:S(2)}, u32[]{:S(2)}) %collective-permute-start.9) | collective-permute-done | bytes 524320 | tf_op jit(solution)/shard_map/ppermute | solution.py:290
  34.1 12.5 %collective-permute-done.10.refs_1_ = bf16[128,2048]{1,0:T(8,128)(2,1)} collective-permute-done((bf16[128,2048]{1,0:T(8,128)(2,1)S(1)}, bf16[128,2048]{1,0:T(8,128)(2,1)}, u32[]{:S(2)}, u32[]{:S(2)}) %collective-permute-start.10) | collective-permute-done | bytes 524320 | tf_op jit(solution)/shard_map/ppermute | solution.py:290
  47.9 2.8 %collective-permute-start.7 = (bf16[256,1024]{1,0:T(8,128)(2,1)S(1)}, bf16[256,1024]{1,0:T(8,128)(2,1)S(1)}, u32[]{:S(2)}, u32[]{:S(2)}) collective-permute-start(bf16[256,1024]{1,0:T(8,128)(2,1)S(1)} %add_convert_fusion.refs_4_), channel_id=1, source_target_pairs={{0,16},{1,17},{2,18},{3,19},{4,20},{5,21},{6,22},{7,23},{8,0},{9,1... | collective-permute-start | bytes 1572872 | tf_op jit(solution)/shard_map/ppermute | solution.py:290
  50.8 3.3 %shard_map.73.refs_0_ = bf16[128,2048]{1,0:T(8,128)(2,1)S(1)} custom-call(bf16[1024,8192]{1,0:T(8,128)(2,1)} %refs_0_.7, f32[8,8,1024]{2,1,0:T(8,128)S(1)} %bitcast.52, bf16[128,1024]{1,0:T(8,128)(2,1)S(1)} %fusion.1.refs_2_), custom_call_target="tpu_custom_call" | custom-call | flops 536870912 | bytes 4194304 | tf_op jit(solution)/shard_map/pallas_call | solution.py:116
  54.2 3.5 %collective-permute-done.1 = s32[1,128]{1,0:T(1,128)S(1)} collective-permute-done((s32[1,128]{1,0:T(1,128)S(1)}, s32[1,128]{1,0:T(1,128)S(1)}, u32[]{:S(2)}, u32[]{:S(2)}) %collective-permute-start.1) | collective-permute-done | bytes 544 | tf_op jit(solution)/shard_map/ppermute | solution.py:290
  57.8 1.5 %collective-permute-start.2 = (s32[1,128]{1,0:T(1,128)S(1)}, s32[1,128]{1,0:T(1,128)S(1)}, u32[]{:S(2)}, u32[]{:S(2)}) collective-permute-start(s32[1,128]{1,0:T(1,128)S(1)} %bitcast.66), channel_id=1, source_target_pairs={{0,4},{1,5},{2,6},{3,7},{4,0},{5,1},{6,2},{7,3},{8,12},{9,13},{10,... | collective-permute-start | bytes 1544 | tf_op jit(solution)/shard_map/ppermute | solution.py:290
  59.3 2.0 %collective-permute-done.2 = s32[1,128]{1,0:T(1,128)S(1)} collective-permute-done((s32[1,128]{1,0:T(1,128)S(1)}, s32[1,128]{1,0:T(1,128)S(1)}, u32[]{:S(2)}, u32[]{:S(2)}) %collective-permute-start.2) | collective-permute-done | bytes 544 | tf_op jit(solution)/shard_map/ppermute | solution.py:290
  64.9 13.0 %collective-permute-done.8.refs_6_ = bf16[256,1024]{1,0:T(8,128)(2,1)S(1)} collective-permute-done((bf16[256,1024]{1,0:T(8,128)(2,1)S(1)}, bf16[256,1024]{1,0:T(8,128)(2,1)S(1)}, u32[]{:S(2)}, u32[]{:S(2)}) %collective-permute-start.8) | collective-permute-done | bytes 524320 | tf_op jit(solution)/shard_map/ppermute | solution.py:290
  77.9 2.8 %near.3 = (f32[256,256]{1,0:T(8,128)S(1)}, bf16[256,1024]{1,0:T(8,128)(2,1)S(1)}, bf16[256,1024]{1,0:T(8,128)(2,1)S(1)}) custom-call(bf16[128,2048]{1,0:T(8,128)(2,1)} %collective-permute-done.9.refs_0_, bf16[128,2048]{1,0:T(8,128)(2,1)} %collective-permute-done.10.refs_1_, bf16[128,2048]{1,0:T(8,128)(2,1)} %collective-permute-done.11.refs_2_, ...), custom_call_target="tpu_custom_call" | custom-call | flops 402653184 | bytes 1572864 | tf_op jit(solution)/shard_map/near/pallas_call | solution.py:191
  80.7 2.3 %near.2 = (f32[256,256]{1,0:T(8,128)S(1)}, bf16[256,1024]{1,0:T(8,128)(2,1)S(1)}, bf16[256,1024]{1,0:T(8,128)(2,1)S(1)}) custom-call(bf16[128,2048]{1,0:T(8,128)(2,1)S(1)} %shard_map.73.refs_0_, bf16[128,2048]{1,0:T(8,128)(2,1)} %collective-permute-done.3.refs_1_, bf16[128,2048]{1,0:T(8,128)(2,1)S(1)} %collective-permute-done.4.refs_2_, ...), custom_call_target="tpu_custom_call" | custom-call | flops 402653184 | bytes 1572864 | tf_op jit(solution)/shard_map/near/pallas_call | solution.py:191
  83.1 5.1 %collective-permute-done.13.refs_7_ = bf16[256,1024]{1,0:T(8,128)(2,1)S(1)} collective-permute-done((bf16[256,1024]{1,0:T(8,128)(2,1)S(1)}, bf16[256,1024]{1,0:T(8,128)(2,1)S(1)}, u32[]{:S(2)}, u32[]{:S(2)}) %collective-permute-start.13) | collective-permute-done | bytes 524320 | tf_op jit(solution)/shard_map/ppermute | solution.py:290
  89.5 2.0 %collective-permute-start.16 = (bf16[256,256]{1,0:T(8,128)(2,1)S(1)}, bf16[256,256]{1,0:T(8,128)(2,1)S(1)}, u32[]{:S(2)}, u32[]{:S(2)}) collective-permute-start(bf16[256,256]{1,0:T(8,128)(2,1)S(1)} %get-tuple-element.31), channel_id=1, source_target_pairs={{0,4},{1,5},{2,6},{3,7},{4,0},{5,1},{6,2},{7,3},{8,12},{9,13},{10,... | collective-permute-start | bytes 393224 | tf_op jit(solution)/shard_map/ppermute | solution.py:290
  91.5 1.4 %collective-permute-start.17 = (bf16[256,256]{1,0:T(8,128)(2,1)S(1)}, bf16[256,256]{1,0:T(8,128)(2,1)S(1)}, u32[]{:S(2)}, u32[]{:S(2)}) collective-permute-start(bf16[256,256]{1,0:T(8,128)(2,1)S(1)} %get-tuple-element.32), channel_id=1, source_target_pairs={{0,6},{1,7},{2,4},{3,5},{4,2},{5,3},{6,0},{7,1},{8,14},{9,15},{10,... | collective-permute-start | bytes 393224 | tf_op jit(solution)/shard_map/ppermute | solution.py:290
  93.2 2.6 %collective-permute-done.15 = bf16[256,256]{1,0:T(8,128)(2,1)S(1)} collective-permute-done((bf16[256,256]{1,0:T(8,128)(2,1)S(1)}, bf16[256,256]{1,0:T(8,128)(2,1)S(1)}, u32[]{:S(2)}, u32[]{:S(2)}) %collective-permute-start.15) | collective-permute-done | bytes 131104 | tf_op jit(solution)/shard_map/ppermute | solution.py:290
  97.0 1.6 %collective-permute-done.17 = bf16[256,256]{1,0:T(8,128)(2,1)S(1)} collective-permute-done((bf16[256,256]{1,0:T(8,128)(2,1)S(1)}, bf16[256,256]{1,0:T(8,128)(2,1)S(1)}, u32[]{:S(2)}, u32[]{:S(2)}) %collective-permute-start.17) | collective-permute-done | bytes 131104 | tf_op jit(solution)/shard_map/ppermute | solution.py:290
  98.8 1.9 %collective-permute-start.19 = (bf16[72,256]{1,0:T(8,128)(2,1)S(1)}, bf16[72,256]{1,0:T(8,128)(2,1)S(1)}, u32[]{:S(2)}, u32[]{:S(2)}) collective-permute-start(bf16[72,256]{1,0:T(8,128)(2,1)S(1)} %pad_maximum_fusion.1), channel_id=1, source_target_pairs={{0,16},{1,17},{2,18},{3,19},{4,20},{5,21},{6,22},{7,23},{8,24},{9,... | collective-permute-start | bytes 110600 | tf_op jit(solution)/shard_map/ppermute | solution.py:290
  100.7 2.5 %collective-permute-start.20 = (bf16[72,256]{1,0:T(8,128)(2,1)S(1)}, bf16[72,256]{1,0:T(8,128)(2,1)S(1)}, u32[]{:S(2)}, u32[]{:S(2)}) collective-permute-start(bf16[72,256]{1,0:T(8,128)(2,1)S(1)} %pad_maximum_fusion.2), channel_id=1, source_target_pairs={{0,24},{1,25},{2,26},{3,27},{4,28},{5,29},{6,30},{7,31},{8,16},{9,... | collective-permute-start | bytes 110600 | tf_op jit(solution)/shard_map/ppermute | solution.py:290
  103.8 2.7 %collective-permute-done.20 = bf16[72,256]{1,0:T(8,128)(2,1)S(1)} collective-permute-done((bf16[72,256]{1,0:T(8,128)(2,1)S(1)}, bf16[72,256]{1,0:T(8,128)(2,1)S(1)}, u32[]{:S(2)}, u32[]{:S(2)}) %collective-permute-start.20) | collective-permute-done | bytes 36896 | tf_op jit(solution)/shard_map/ppermute | solution.py:290
  (66 shorter events, 10.0 us)
Async XLA Ops:
  0.0 13.4 %copy-start.1 = (s32[1,1024]{1,0:T(1,128)S(1)}, s32[1,1024]{1,0:T(1,128)}, u32[]{:S(2)}) copy-start(s32[1,1024]{1,0:T(1,128)} %param.9) | copy-start | bytes 12292
  0.0 13.4 %copy-start = (f32[64,1024]{1,0:T(8,128)S(1)}, f32[64,1024]{1,0:T(8,128)}, u32[]{:S(2)}) copy-start(f32[64,1024]{1,0:T(8,128)} %param.8) | copy-start | bytes 786436
  12.8 33.8 %collective-permute-start.6 = (f32[256,1024]{1,0:T(8,128)}, f32[256,1024]{1,0:T(8,128)}, u32[]{:S(2)}, u32[]{:S(2)}) collective-permute-start(f32[256,1024]{1,0:T(8,128)} %get-tuple-element.20), channel_id=1, source_target_pairs={{0,1},{1,0},{2,3},{3,2},{4,5},{5,4},{6,7},{7,6},{8,9},{9,8},{10,11... | collective-permute-start | bytes 3145736 | tf_op jit(solution)/shard_map/ppermute | solution.py:290
  18.6 15.4 %collective-permute-start.9 = (bf16[128,2048]{1,0:T(8,128)(2,1)S(1)}, bf16[128,2048]{1,0:T(8,128)(2,1)}, u32[]{:S(2)}, u32[]{:S(2)}) collective-permute-start(bf16[128,2048]{1,0:T(8,128)(2,1)S(1)} %get-tuple-element.22), channel_id=1, source_target_pairs={{0,2},{1,3},{2,0},{3,1},{4,6},{5,7},{6,4},{7,5},{8,10},{9,11},{10,... | collective-permute-start | bytes 1572872 | tf_op jit(solution)/shard_map/ppermute | solution.py:290
  21.2 25.4 %collective-permute-start.10 = (bf16[128,2048]{1,0:T(8,128)(2,1)S(1)}, bf16[128,2048]{1,0:T(8,128)(2,1)}, u32[]{:S(2)}, u32[]{:S(2)}) collective-permute-start(bf16[128,2048]{1,0:T(8,128)(2,1)S(1)} %get-tuple-element.23), channel_id=1, source_target_pairs={{0,4},{1,5},{2,6},{3,7},{4,0},{5,1},{6,2},{7,3},{8,12},{9,13},{10,... | collective-permute-start | bytes 1572872 | tf_op jit(solution)/shard_map/ppermute | solution.py:290
  22.7 28.0 %copy-start.3 = (s32[4]{0:T(128)S(1)}, s32[4]{0:T(128)}, u32[]{:S(2)}) copy-start(s32[4]{0:T(128)} %constant.106.clone) | copy-start | bytes 52
  22.7 31.4 %collective-permute-start = (s32[1,128]{1,0:T(1,128)S(1)}, s32[1,128]{1,0:T(1,128)S(1)}, u32[]{:S(2)}, u32[]{:S(2)}) collective-permute-start(s32[1,128]{1,0:T(1,128)S(1)} %bitcast.64), channel_id=1, source_target_pairs={{0,6},{1,7},{2,4},{3,5},{4,2},{5,3},{6,0},{7,1},{8,14},{9,15},{10,... | collective-permute-start | bytes 1544 | tf_op jit(solution)/shard_map/ppermute | solution.py:290
  26.9 34.7 %collective-permute-start.3 = (bf16[128,2048]{1,0:T(8,128)(2,1)}, bf16[128,2048]{1,0:T(8,128)(2,1)}, u32[]{:S(2)}, u32[]{:S(2)}) collective-permute-start(bf16[128,2048]{1,0:T(8,128)(2,1)} %shard_map.74), channel_id=1, source_target_pairs={{0,6},{1,7},{2,4},{3,5},{4,2},{5,3},{6,0},{7,1},{8,14},{9,15},{10,... | collective-permute-start | bytes 1572872 | tf_op jit(solution)/shard_map/ppermute | solution.py:290
  34.1 28.1 %collective-permute-start.11 = (bf16[128,2048]{1,0:T(8,128)(2,1)}, bf16[128,2048]{1,0:T(8,128)(2,1)}, u32[]{:S(2)}, u32[]{:S(2)}) collective-permute-start(bf16[128,2048]{1,0:T(8,128)(2,1)} %collective-permute-done.9.refs_0_), channel_id=1, source_target_pairs={{0,1},{1,0},{2,3},{3,2},{4,5},{5,4},{6,7},{7,6},{8,9},{9,8},{10,11... | collective-permute-start | bytes 1572872 | tf_op jit(solution)/shard_map/ppermute | solution.py:290
  46.6 15.6 %collective-permute-start.12 = (bf16[128,2048]{1,0:T(8,128)(2,1)}, bf16[128,2048]{1,0:T(8,128)(2,1)}, u32[]{:S(2)}, u32[]{:S(2)}) collective-permute-start(bf16[128,2048]{1,0:T(8,128)(2,1)} %collective-permute-done.10.refs_1_), channel_id=1, source_target_pairs={{0,1},{1,0},{2,3},{3,2},{4,5},{5,4},{6,7},{7,6},{8,9},{9,8},{10,11... | collective-permute-start | bytes 1572872 | tf_op jit(solution)/shard_map/ppermute | solution.py:290
  47.9 14.9 %collective-permute-start.7 = (bf16[256,1024]{1,0:T(8,128)(2,1)S(1)}, bf16[256,1024]{1,0:T(8,128)(2,1)S(1)}, u32[]{:S(2)}, u32[]{:S(2)}) collective-permute-start(bf16[256,1024]{1,0:T(8,128)(2,1)S(1)} %add_convert_fusion.refs_4_), channel_id=1, source_target_pairs={{0,16},{1,17},{2,18},{3,19},{4,20},{5,21},{6,22},{7,23},{8,0},{9,1... | collective-permute-start | bytes 1572872 | tf_op jit(solution)/shard_map/ppermute | solution.py:290
  54.1 3.6 %collective-permute-start.1 = (s32[1,128]{1,0:T(1,128)S(1)}, s32[1,128]{1,0:T(1,128)S(1)}, u32[]{:S(2)}, u32[]{:S(2)}) collective-permute-start(s32[1,128]{1,0:T(1,128)S(1)} %bitcast.65), channel_id=1, source_target_pairs={{0,2},{1,3},{2,0},{3,1},{4,6},{5,7},{6,4},{7,5},{8,10},{9,11},{10,... | collective-permute-start | bytes 1544 | tf_op jit(solution)/shard_map/ppermute | solution.py:290
  57.8 3.6 %collective-permute-start.2 = (s32[1,128]{1,0:T(1,128)S(1)}, s32[1,128]{1,0:T(1,128)S(1)}, u32[]{:S(2)}, u32[]{:S(2)}) collective-permute-start(s32[1,128]{1,0:T(1,128)S(1)} %bitcast.66), channel_id=1, source_target_pairs={{0,4},{1,5},{2,6},{3,7},{4,0},{5,1},{6,2},{7,3},{8,12},{9,13},{10,... | collective-permute-start | bytes 1544 | tf_op jit(solution)/shard_map/ppermute | solution.py:290
  61.3 19.4 %collective-permute-start.4 = (bf16[128,2048]{1,0:T(8,128)(2,1)S(1)}, bf16[128,2048]{1,0:T(8,128)(2,1)S(1)}, u32[]{:S(2)}, u32[]{:S(2)}) collective-permute-start(bf16[128,2048]{1,0:T(8,128)(2,1)S(1)} %shard_map.73.refs_0_), channel_id=1, source_target_pairs={{0,1},{1,0},{2,3},{3,2},{4,5},{5,4},{6,7},{7,6},{8,9},{9,8},{10,11... | collective-permute-start | bytes 1572872 | tf_op jit(solution)/shard_map/ppermute | solution.py:290
  61.6 19.1 %collective-permute-start.5 = (bf16[128,2048]{1,0:T(8,128)(2,1)}, bf16[128,2048]{1,0:T(8,128)(2,1)S(1)}, u32[]{:S(2)}, u32[]{:S(2)}) collective-permute-start(bf16[128,2048]{1,0:T(8,128)(2,1)} %collective-permute-done.3.refs_1_), channel_id=1, source_target_pairs={{0,1},{1,0},{2,3},{3,2},{4,5},{5,4},{6,7},{7,6},{8,9},{9,8},{10,11... | collective-permute-start | bytes 1572872 | tf_op jit(solution)/shard_map/ppermute | solution.py:290
  62.2 15.7 %collective-permute-start.8 = (bf16[256,1024]{1,0:T(8,128)(2,1)S(1)}, bf16[256,1024]{1,0:T(8,128)(2,1)S(1)}, u32[]{:S(2)}, u32[]{:S(2)}) collective-permute-start(bf16[256,1024]{1,0:T(8,128)(2,1)S(1)} %add_convert_fusion.refs_4_), channel_id=1, source_target_pairs={{0,8},{1,9},{2,10},{3,11},{4,12},{5,13},{6,14},{7,15},{8,24},{9,25... | collective-permute-start | bytes 1572872 | tf_op jit(solution)/shard_map/ppermute | solution.py:290
  62.2 20.9 %collective-permute-start.14 = (bf16[256,1024]{1,0:T(8,128)(2,1)S(1)}, bf16[256,1024]{1,0:T(8,128)(2,1)S(1)}, u32[]{:S(2)}, u32[]{:S(2)}) collective-permute-start(bf16[256,1024]{1,0:T(8,128)(2,1)S(1)} %add_convert_fusion.refs_4_), channel_id=1, source_target_pairs={{8,16},{9,17},{10,18},{11,19},{12,20},{13,21},{14,22},{15,23},{16,... | collective-permute-start | bytes 1572872 | tf_op jit(solution)/shard_map/ppermute | solution.py:290
  62.9 25.3 %collective-permute-start.13 = (bf16[256,1024]{1,0:T(8,128)(2,1)S(1)}, bf16[256,1024]{1,0:T(8,128)(2,1)S(1)}, u32[]{:S(2)}, u32[]{:S(2)}) collective-permute-start(bf16[256,1024]{1,0:T(8,128)(2,1)S(1)} %collective-permute-done.7.refs_5_), channel_id=1, source_target_pairs={{8,0},{9,1},{10,2},{11,3},{12,4},{13,5},{14,6},{15,7},{16,24},{17,... | collective-permute-start | bytes 1572872 | tf_op jit(solution)/shard_map/ppermute | solution.py:290
  89.4 6.4 %collective-permute-start.15 = (bf16[256,256]{1,0:T(8,128)(2,1)S(1)}, bf16[256,256]{1,0:T(8,128)(2,1)S(1)}, u32[]{:S(2)}, u32[]{:S(2)}) collective-permute-start(bf16[256,256]{1,0:T(8,128)(2,1)S(1)} %get-tuple-element.30), channel_id=1, source_target_pairs={{0,2},{1,3},{2,0},{3,1},{4,6},{5,7},{6,4},{7,5},{8,10},{9,11},{10,... | collective-permute-start | bytes 393224 | tf_op jit(solution)/shard_map/ppermute | solution.py:290
  89.5 7.5 %collective-permute-start.16 = (bf16[256,256]{1,0:T(8,128)(2,1)S(1)}, bf16[256,256]{1,0:T(8,128)(2,1)S(1)}, u32[]{:S(2)}, u32[]{:S(2)}) collective-permute-start(bf16[256,256]{1,0:T(8,128)(2,1)S(1)} %get-tuple-element.31), channel_id=1, source_target_pairs={{0,4},{1,5},{2,6},{3,7},{4,0},{5,1},{6,2},{7,3},{8,12},{9,13},{10,... | collective-permute-start | bytes 393224 | tf_op jit(solution)/shard_map/ppermute | solution.py:290
  91.5 7.1 %collective-permute-start.17 = (bf16[256,256]{1,0:T(8,128)(2,1)S(1)}, bf16[256,256]{1,0:T(8,128)(2,1)S(1)}, u32[]{:S(2)}, u32[]{:S(2)}) collective-permute-start(bf16[256,256]{1,0:T(8,128)(2,1)S(1)} %get-tuple-element.32), channel_id=1, source_target_pairs={{0,6},{1,7},{2,4},{3,5},{4,2},{5,3},{6,0},{7,1},{8,14},{9,15},{10,... | collective-permute-start | bytes 393224 | tf_op jit(solution)/shard_map/ppermute | solution.py:290
  98.7 4.5 %collective-permute-start.18 = (bf16[72,256]{1,0:T(8,128)(2,1)S(1)}, bf16[72,256]{1,0:T(8,128)(2,1)S(1)}, u32[]{:S(2)}, u32[]{:S(2)}) collective-permute-start(bf16[72,256]{1,0:T(8,128)(2,1)S(1)} %pad_maximum_fusion), channel_id=1, source_target_pairs={{0,8},{1,9},{2,10},{3,11},{4,12},{5,13},{6,14},{7,15},{8,0},{9,1},... | collective-permute-start | bytes 110600 | tf_op jit(solution)/shard_map/ppermute | solution.py:290
  98.8 4.9 %collective-permute-start.19 = (bf16[72,256]{1,0:T(8,128)(2,1)S(1)}, bf16[72,256]{1,0:T(8,128)(2,1)S(1)}, u32[]{:S(2)}, u32[]{:S(2)}) collective-permute-start(bf16[72,256]{1,0:T(8,128)(2,1)S(1)} %pad_maximum_fusion.1), channel_id=1, source_target_pairs={{0,16},{1,17},{2,18},{3,19},{4,20},{5,21},{6,22},{7,23},{8,24},{9,... | collective-permute-start | bytes 110600 | tf_op jit(solution)/shard_map/ppermute | solution.py:290
  100.7 5.8 %collective-permute-start.20 = (bf16[72,256]{1,0:T(8,128)(2,1)S(1)}, bf16[72,256]{1,0:T(8,128)(2,1)S(1)}, u32[]{:S(2)}, u32[]{:S(2)}) collective-permute-start(bf16[72,256]{1,0:T(8,128)(2,1)S(1)} %pad_maximum_fusion.2), channel_id=1, source_target_pairs={{0,24},{1,25},{2,26},{3,27},{4,28},{5,29},{6,30},{7,31},{8,16},{9,... | collective-permute-start | bytes 110600 | tf_op jit(solution)/shard_map/ppermute | solution.py:290
  (1 other events, 9.3 us)
